TPU v7x, 512 devices: a whole 4x8x8 slice. The times are simulated.
512 devices in a mesh: rows: 16 (over x_lo, z), cols: 32 (over y, x_hi, core).
Axes of the slice: x: 4 (x_hi: 2, x_lo: 2; x = x_hi * 2 + x_lo), y: 8, z: 8, core: 2. Of those that a mesh axis runs over, the one named last changes fastest.
Arguments:
- tokens: bfloat16 [128, 1024, 192], P('rows', 'cols'), may hold values from -60 to 60
- region_ids: int32 [128, 1024], P('rows', 'cols'), may hold values from 0 to 2
- upper_rim: bfloat16 [4, 1024, 192], P(None, 'cols'), may hold values from -60 to 60
- upper_ids: int32 [4, 1024], P(None, 'cols'), may hold values from 0 to 2
- lower_rim: bfloat16 [4, 1024, 192], P(None, 'cols'), may hold values from -60 to 60
- lower_ids: int32 [4, 1024], P(None, 'cols'), may hold values from 0 to 2
- cotangent: bfloat16 [128, 1024, 192], P('rows', 'cols'), may hold values from -6 to 6
- qkv_weight: bfloat16 [2, 192, 576], replicated, may hold values from -0.4375 to 0.4375
- proj_weight: bfloat16 [2, 192, 192], replicated, may hold values from -0.4375 to 0.4375
- inner_weight: bfloat16 [2, 192, 768], replicated, may hold values from -0.4375 to 0.4375
- outer_weight: bfloat16 [2, 768, 192], replicated, may hold values from -0.21875 to 0.21875
- bias_table: float32 [2, 225, 6], replicated, may hold values from -4 to 400
Outputs:
- token_grad: bfloat16 [128, 1024, 192], P('rows', 'cols')
- qkv_grad: float32 [2, 192, 576], P(None, 'rows', 'cols')
- proj_grad: float32 [2, 192, 192], P(None, 'rows', 'cols')
- inner_grad: float32 [2, 192, 768], P(None, 'rows', 'cols')
- outer_grad: float32 [2, 768, 192], P(None, 'rows', 'cols')
- table_grad: float32 [2, 225, 6], replicated
All inputs are finite; a program needn't handle non-finite values.
Results may differ from a plain program's by a relative error of at most 0.03.
Values may be sent and summed in bfloat16 or wider, within the bound.
A program may use at most 64 MiB of HBM per device.

v0:
```python
import jax
import jax.numpy as jnp
from jax import lax
from jax.sharding import PartitionSpec as P

WIN = 8
HALF = 4
BIAS_LEN = 225
EPS = 1e-05
MASKED = -1000000000.0


def with_halo(block, sides, width, periodic):
    for axis, dim in sides:
        count = lax.axis_size(axis)
        forward = [(i, i + 1) for i in range(count - 1)]
        if periodic:
            forward.append((count - 1, 0))
        backward = [(target, source) for source, target in forward]
        low = lax.ppermute(
            lax.slice_in_dim(block, block.shape[dim] - width, None, axis=dim), axis, forward
        )
        high = lax.ppermute(lax.slice_in_dim(block, 0, width, axis=dim), axis, backward)
        block = jnp.concatenate([low, block, high], axis=dim)
    return block


def normalize(values):
    center = jnp.mean(values, axis=-1, keepdims=True)
    shifted = values - center
    spread = jnp.mean(shifted * shifted, axis=-1, keepdims=True)
    return shifted * lax.rsqrt(spread + EPS)


def norm_back(source, grad_norm):
    _, pullback = jax.vjp(normalize, source.astype(jnp.float32))
    return pullback(grad_norm)[0]


def by_transpose(left, right):
    return lax.dot_general(
        left, right, (((1,), (1,)), ((), ())), preferred_element_type=jnp.float32
    )


def over_rows(left, right):
    return lax.dot_general(
        left, right, (((0,), (0,)), ((), ())), preferred_element_type=jnp.float32
    )


def windows(surface):
    grid_rows, grid_cols = (surface.shape[0], surface.shape[1])
    trailing = surface.shape[2:]
    blocked = surface.reshape((grid_rows // WIN, WIN, grid_cols // WIN, WIN) + trailing)
    permute = (0, 2, 1, 3) + tuple(range(4, 4 + len(trailing)))
    return blocked.transpose(permute).reshape(
        (grid_rows // WIN * (grid_cols // WIN), WIN * WIN) + trailing
    )


def unwindows(framed, grid_rows, grid_cols):
    trailing = framed.shape[2:]
    blocked = framed.reshape((grid_rows // WIN, grid_cols // WIN, WIN, WIN) + trailing)
    permute = (0, 2, 1, 3) + tuple(range(4, 4 + len(trailing)))
    return blocked.transpose(permute).reshape((grid_rows, grid_cols) + trailing)


def relative_onehot():
    places = jnp.arange(WIN * WIN, dtype=jnp.int32)
    pos_row = places // WIN
    pos_col = places % WIN
    lookup = (
        (pos_row[:, None] - pos_row[None, :] + WIN - 1) * (2 * WIN - 1)
        + pos_col[:, None]
        - pos_col[None, :]
        + WIN
        - 1
    )
    return (lookup[:, :, None] == jnp.arange(BIAS_LEN, dtype=jnp.int32)[None, None, :]).astype(
        jnp.float32
    )


def attend(normed_win, ids_win, qkv_weight, pos_bias):
    window_count, window_size, channels = normed_win.shape
    head_count = pos_bias.shape[0]
    head_size = channels // head_count
    score_scale = head_size ** (-0.5)
    qkv_all = jnp.dot(
        normed_win.reshape(window_count * window_size, channels),
        qkv_weight,
        preferred_element_type=jnp.float32,
    )
    qkv_all = qkv_all.astype(jnp.bfloat16).reshape(
        window_count, window_size, 3, head_count, head_size
    )
    scores = jnp.einsum(
        "nqhd,nkhd->nhqk", qkv_all[:, :, 0], qkv_all[:, :, 1], preferred_element_type=jnp.float32
    )
    scores = scores * score_scale + pos_bias[None]
    same_region = ids_win[:, :, None] == ids_win[:, None, :]
    scores = jnp.where(same_region[:, None], scores, MASKED)
    row_max = jnp.max(scores, axis=-1, keepdims=True)
    exponent = jnp.exp(scores - row_max)
    attn_probs = exponent / jnp.sum(exponent, axis=-1, keepdims=True)
    attn_out = jnp.einsum(
        "nhqk,nkhd->nqhd",
        attn_probs.astype(jnp.bfloat16),
        qkv_all[:, :, 2],
        preferred_element_type=jnp.float32,
    )
    return (
        qkv_all,
        attn_probs,
        attn_out.astype(jnp.bfloat16).reshape(window_count, window_size, channels),
    )


def attend_back(normed_win, qkv_all, attn_probs, grad_out, qkv_weight):
    window_count, window_size, channels = normed_win.shape
    head_count, head_size = (qkv_all.shape[3], qkv_all.shape[4])
    score_scale = head_size ** (-0.5)
    grad_heads = grad_out.reshape(window_count, window_size, head_count, head_size)
    grad_probs = jnp.einsum(
        "nqhd,nkhd->nhqk", grad_heads, qkv_all[:, :, 2], preferred_element_type=jnp.float32
    )
    grad_scores = attn_probs * (
        grad_probs - jnp.sum(grad_probs * attn_probs, axis=-1, keepdims=True)
    )
    grad_bias = jnp.sum(grad_scores, axis=0)
    scores_low = grad_scores.astype(jnp.bfloat16)
    grad_query = (
        jnp.einsum(
            "nhqk,nkhd->nqhd", scores_low, qkv_all[:, :, 1], preferred_element_type=jnp.float32
        )
        * score_scale
    )
    grad_key = (
        jnp.einsum(
            "nhqk,nqhd->nkhd", scores_low, qkv_all[:, :, 0], preferred_element_type=jnp.float32
        )
        * score_scale
    )
    grad_value = jnp.einsum(
        "nhqk,nqhd->nkhd",
        attn_probs.astype(jnp.bfloat16),
        grad_heads,
        preferred_element_type=jnp.float32,
    )
    grad_qkv = jnp.stack([grad_query, grad_key, grad_value], axis=2).astype(jnp.bfloat16)
    grad_qkv = grad_qkv.reshape(window_count * window_size, 3 * channels)
    flattened = normed_win.reshape(window_count * window_size, channels)
    grad_norm = by_transpose(grad_qkv, qkv_weight)
    grad_weight = over_rows(flattened, grad_qkv)
    return (grad_norm.reshape(window_count, window_size, channels), grad_weight, grad_bias)


def mixer_forward(surface, region, qkv_weight, table):
    grid_rows, grid_cols = (surface.shape[0], surface.shape[1])
    normed = normalize(surface.astype(jnp.float32)).astype(jnp.bfloat16)
    pos_bias = jnp.einsum("ijb,bh->hij", relative_onehot(), table, precision=lax.Precision.HIGHEST)
    qkv_all, attn_probs, attn_out = attend(windows(normed), windows(region), qkv_weight, pos_bias)
    return (normed, qkv_all, attn_probs, unwindows(attn_out, grid_rows, grid_cols))


def mixer_backward(surface, normed, qkv_all, attn_probs, grad_mix, qkv_weight):
    grid_rows, grid_cols = (surface.shape[0], surface.shape[1])
    grad_norm, grad_weight, grad_bias = attend_back(
        windows(normed), qkv_all, attn_probs, windows(grad_mix), qkv_weight
    )
    grad_surface = norm_back(surface, unwindows(grad_norm, grid_rows, grid_cols))
    grad_table = jnp.einsum(
        "ijb,hij->bh", relative_onehot(), grad_bias, precision=lax.Precision.HIGHEST
    )
    return (grad_surface, grad_weight, grad_table)


def channel_forward(middle, inner_w, outer_w):
    normed = normalize(middle.astype(jnp.float32)).astype(jnp.bfloat16)
    hidden_pre = jnp.dot(normed, inner_w, preferred_element_type=jnp.float32)
    hidden_act = jax.nn.gelu(hidden_pre, approximate=False).astype(jnp.bfloat16)
    output = (
        middle.astype(jnp.float32)
        + jnp.dot(hidden_act, outer_w, preferred_element_type=jnp.float32)
    ).astype(jnp.bfloat16)
    return (normed, hidden_pre, hidden_act, output)


def channel_backward(middle, normed, hidden_pre, hidden_act, grad_out, inner_w, outer_w):
    grad_act = by_transpose(grad_out, outer_w)
    grad_outer = over_rows(hidden_act, grad_out)
    _, pullback = jax.vjp(lambda inputs: jax.nn.gelu(inputs, approximate=False), hidden_pre)
    grad_pre = pullback(grad_act)[0].astype(jnp.bfloat16)
    grad_norm = by_transpose(grad_pre, inner_w)
    grad_inner = over_rows(normed, grad_pre)
    grad_middle = (grad_out.astype(jnp.float32) + norm_back(middle, grad_norm)).astype(jnp.bfloat16)
    return (grad_middle, grad_inner, grad_outer)


def fold_rims(grad_ext):
    col_edges = jnp.concatenate([grad_ext[:, :HALF], grad_ext[:, -HALF:]], axis=1)
    col_recv = with_halo(col_edges.astype(jnp.bfloat16), (("cols", 1),), HALF, True).astype(
        col_edges.dtype
    )
    center = grad_ext[:, HALF:-HALF]
    center = jnp.concatenate(
        [
            center[:, :HALF] + col_recv[:, :HALF],
            center[:, HALF:-HALF],
            center[:, -HALF:] + col_recv[:, -HALF:],
        ],
        axis=1,
    )
    row_edges = jnp.concatenate([center[:HALF], center[-HALF:]], axis=0)
    row_recv = with_halo(row_edges.astype(jnp.bfloat16), (("rows", 0),), HALF, False).astype(
        row_edges.dtype
    )
    interior = center[HALF:-HALF]
    return jnp.concatenate(
        [
            interior[:HALF] + row_recv[:HALF],
            interior[HALF:-HALF],
            interior[-HALF:] + row_recv[-HALF:],
        ],
        axis=0,
    )


def reduce_grads(qkv_term, proj_term, inner_term, outer_term):
    row_count = lax.axis_size("rows")
    col_count = lax.axis_size("cols")
    tile_count = row_count * col_count
    reduced = (
        lax.psum_scatter(
            qkv_term.astype(jnp.bfloat16), "cols", scatter_dimension=1, tiled=True
        ).astype(jnp.float32),
        lax.psum_scatter(
            proj_term.astype(jnp.bfloat16), "cols", scatter_dimension=1, tiled=True
        ).astype(jnp.float32),
        lax.psum_scatter(
            inner_term.astype(jnp.bfloat16), "cols", scatter_dimension=1, tiled=True
        ).astype(jnp.float32),
        lax.psum_scatter(
            outer_term.astype(jnp.bfloat16), "cols", scatter_dimension=1, tiled=True
        ).astype(jnp.float32),
    )
    reduced = (
        lax.psum_scatter(
            reduced[0].astype(jnp.bfloat16), "rows", scatter_dimension=0, tiled=True
        ).astype(jnp.float32),
        lax.psum_scatter(
            reduced[1].astype(jnp.bfloat16), "rows", scatter_dimension=0, tiled=True
        ).astype(jnp.float32),
        lax.psum_scatter(
            reduced[2].astype(jnp.bfloat16), "rows", scatter_dimension=0, tiled=True
        ).astype(jnp.float32),
        lax.psum_scatter(
            reduced[3].astype(jnp.bfloat16), "rows", scatter_dimension=0, tiled=True
        ).astype(jnp.float32),
    )
    return tuple((section / tile_count for section in reduced))


def local(
    tokens,
    region_ids,
    upper_rim,
    upper_ids,
    lower_rim,
    lower_ids,
    cotangent,
    qkv_weight,
    proj_weight,
    inner_weight,
    outer_weight,
    bias_table,
):
    tile_rows, tile_cols, channels = tokens.shape
    row_index = lax.axis_index("rows")
    row_count = lax.axis_size("rows")
    tile_count = row_count * lax.axis_size("cols")
    normed_one, qkv_one, probs_one, mix_one = mixer_forward(
        tokens, region_ids, qkv_weight[0], bias_table[0]
    )
    mix_flat_one = mix_one.reshape(tile_rows * tile_cols, channels)
    middle_one = (
        tokens.reshape(-1, channels).astype(jnp.float32)
        + jnp.dot(mix_flat_one, proj_weight[0], preferred_element_type=jnp.float32)
    ).astype(jnp.bfloat16)
    chan_one = channel_forward(middle_one, inner_weight[0], outer_weight[0])
    first_out = chan_one[3].reshape(tile_rows, tile_cols, channels)
    region_low = region_ids.astype(jnp.bfloat16)
    row_ext, row_ids = (
        with_halo(first_out, (("rows", 0),), HALF, False),
        with_halo(region_low, (("rows", 0),), HALF, False),
    )
    at_top = row_index == 0
    at_bottom = row_index == row_count - 1
    row_ext = jnp.concatenate(
        [
            jnp.where(at_top, upper_rim, row_ext[:HALF]),
            row_ext[HALF:-HALF],
            jnp.where(at_bottom, lower_rim, row_ext[-HALF:]),
        ],
        axis=0,
    )
    row_ids = jnp.concatenate(
        [
            jnp.where(at_top, upper_ids.astype(jnp.bfloat16), row_ids[:HALF]),
            row_ids[HALF:-HALF],
            jnp.where(at_bottom, lower_ids.astype(jnp.bfloat16), row_ids[-HALF:]),
        ],
        axis=0,
    )
    extended, ext_ids = (
        with_halo(row_ext, (("cols", 1),), HALF, True),
        with_halo(row_ids, (("cols", 1),), HALF, True),
    )
    ext_region = ext_ids.astype(jnp.int32)
    normed_two, qkv_two, probs_two, mix_ext = mixer_forward(
        extended, ext_region, qkv_weight[1], bias_table[1]
    )
    mix_flat_two = mix_ext[HALF : HALF + tile_rows, HALF : HALF + tile_cols].reshape(
        tile_rows * tile_cols, channels
    )
    middle_two = (
        chan_one[3].astype(jnp.float32)
        + jnp.dot(mix_flat_two, proj_weight[1], preferred_element_type=jnp.float32)
    ).astype(jnp.bfloat16)
    chan_two = channel_forward(middle_two, inner_weight[1], outer_weight[1])
    grad_out = cotangent.reshape(-1, channels)
    grad_mid_two, inner_two, outer_two = channel_backward(
        middle_two,
        chan_two[0],
        chan_two[1],
        chan_two[2],
        grad_out,
        inner_weight[1],
        outer_weight[1],
    )
    proj_two = over_rows(mix_flat_two, grad_mid_two)
    grad_mix_two = (
        by_transpose(grad_mid_two, proj_weight[1])
        .astype(jnp.bfloat16)
        .reshape(tile_rows, tile_cols, channels)
    )
    grad_mix_ext = jnp.pad(grad_mix_two, ((HALF, HALF), (HALF, HALF), (0, 0)))
    grad_ext, qkv_two_grad, table_two = mixer_backward(
        extended, normed_two, qkv_two, probs_two, grad_mix_ext, qkv_weight[1]
    )
    folded = fold_rims(grad_ext)
    grad_first = (
        grad_mid_two.reshape(tile_rows, tile_cols, channels).astype(jnp.float32) + folded
    ).astype(jnp.bfloat16)
    summed_two = reduce_grads(qkv_two_grad, proj_two, inner_two, outer_two)
    grad_mid_one, inner_one, outer_one = channel_backward(
        middle_one,
        chan_one[0],
        chan_one[1],
        chan_one[2],
        grad_first.reshape(-1, channels),
        inner_weight[0],
        outer_weight[0],
    )
    proj_one = over_rows(mix_flat_one, grad_mid_one)
    grad_mix_one = (
        by_transpose(grad_mid_one, proj_weight[0])
        .astype(jnp.bfloat16)
        .reshape(tile_rows, tile_cols, channels)
    )
    grad_tokens, qkv_one_grad, table_one = mixer_backward(
        tokens, normed_one, qkv_one, probs_one, grad_mix_one, qkv_weight[0]
    )
    token_grad = (
        grad_mid_one.reshape(tile_rows, tile_cols, channels).astype(jnp.float32) + grad_tokens
    ).astype(jnp.bfloat16)
    summed_one = reduce_grads(qkv_one_grad, proj_one, inner_one, outer_one)
    table_sum = lax.psum(jnp.stack([table_one, table_two]), ("rows", "cols"))
    qkv_grad = jnp.stack([summed_one[0], summed_two[0]])
    proj_grad = jnp.stack([summed_one[1], summed_two[1]])
    inner_grad = jnp.stack([summed_one[2], summed_two[2]])
    outer_grad = jnp.stack([summed_one[3], summed_two[3]])
    return (token_grad, qkv_grad, proj_grad, inner_grad, outer_grad, table_sum / tile_count)


def solution(mesh):
    return jax.shard_map(
        local,
        mesh=mesh,
        in_specs=(
            P("rows", "cols", None),
            P("rows", "cols"),
            P(None, "cols", None),
            P(None, "cols"),
            P(None, "cols", None),
            P(None, "cols"),
            P("rows", "cols", None),
            P(),
            P(),
            P(),
            P(),
            P(),
        ),
        out_specs=(
            P("rows", "cols", None),
            P(None, "rows", "cols"),
            P(None, "rows", "cols"),
            P(None, "rows", "cols"),
            P(None, "rows", "cols"),
            P(),
        ),
        check_vma=False,
    )
```

profile of v0, /device:TPU:16, one launch (start us, length us, event | category | flops | bytes accessed | tf_op | source)
XLA Modules:
  0.0 740.8 jit_solution(4633801604680968060)
XLA Ops:
  8.5 4.8 collective-permute-start.4
  22.0 2.6 fusion.29
  27.7 2.9 multiply_convert_fusion.1
  33.3 5.2 collective-permute-start
  38.6 2.6 fusion.30
  44.7 6.0 collective-permute-start.7
  52.6 4.1 collective-permute-start.2
  56.7 3.9 collective-permute-start.3
  64.6 3.2 reshape.352
  69.5 2.5 fusion.136
  73.2 2.3 fusion.23
  78.5 2.8 fusion.47
  85.6 2.3 fusion.24
  91.9 2.5 copy.166
  94.4 4.0 copy.147
  98.4 5.6 convert_element_type.304
  104.0 2.6 multiply_reduce_fusion.2
  108.8 2.0 convert_element_type.320
  110.8 2.3 convolution_convert_fusion.9
  115.4 3.2 collective-permute-start.8
  118.7 4.7 collective-permute-start.9
  125.2 4.7 collective-permute-start.10
  132.0 6.0 collective-permute-done.11
  138.6 2.0 add_convert_fusion
  146.3 68.5 %fusion.122 = (bf16[192,24]{0,1:T(8,128)(2,1)S(1)}, bf16[192,24]{0,1:T(8,128)(2,1)S(1)}, bf16[192,8]{0,1:T(8,128)(2,1)S(1)}, bf16[192,8]{0,1:T(8,128)(2,1)S(1)},...) fusion(bf16[192,576]{0,1:T(8,128)(2,1)} %convolution_convert_fusion.9, ...), kind=kCustom, calls=%all-reduce-scatter.6 | all-reduce-scatter fusion | flops 786434 | bytes 1230848
  214.8 20.4 %collective-permute-start.51 = (bf16[768,6]{0,1:T(8,128)(2,1)S(1)}, bf16[768,6]{0,1:T(8,128)(2,1)S(1)}, u32[]{:S(2)}, u32[]{:S(2)}) collective-permute-start(bf16[768,6]{0,1:T(8,128)(2,1)S(1)} %slice.212), channel_id=1, source_target_pairs={{0,8},{1,9},{2,10},{3,11},{4,12},{5,13},{6,14},{7,15},{8,16},{9,17... | collective-permute-start | bytes 27656
  235.2 1.9 collective-permute-start.50
  237.2 1.9 collective-permute-start.49
  239.1 1.9 collective-permute-start.48
  241.0 1.9 collective-permute-start.47
  243.0 4.6 collective-permute-start.46
  252.1 1.9 collective-permute-start.58
  254.0 1.9 collective-permute-start.57
  256.0 2.2 collective-permute-start.45
  260.1 1.9 collective-permute-start.59
  268.8 3.1 collective-permute-start.54
  271.9 3.3 collective-permute-start.53
  279.9 2.8 collective-permute-done.52
  287.5 2.1 collective-permute-start.42
  302.3 1.9 collective-permute-start.39
  304.3 4.6 collective-permute-start.38
  308.9 2.2 collective-permute-start.37
  311.1 2.1 collective-permute-start.36
  313.2 4.2 collective-permute-start.34
  319.4 1.9 collective-permute-start.32
  321.4 104.6 %psum.7 = f32[2,225,6]{1,2,0:T(8,128)S(1)} all-reduce(f32[2,225,6]{1,2,0:T(8,128)S(1)} %pad_maximum_fusion.16), channel_id=1, replica_groups=mesh['rows'=16,'cols'=32] {'rows','cols'}, use_global_device_ids=true, to_apply=%region_40.41 | all-reduce | flops 2700 | bytes 21600 | tf_op jit(solution)/shard_map/psum | solution.py:379
  426.0 3.2 collective-permute-start.31
  431.1 4.8 collective-permute-start.29
  437.9 4.4 collective-permute-start.27
  443.7 5.6 collective-permute-start.26
  449.3 3.9 collective-permute-start.25
  453.3 1.9 collective-permute-start.24
  457.2 2.8 collective-permute-start.22
  460.9 2.8 collective-permute-start.21
  465.6 3.3 collective-permute-start.18
  474.8 1.9 collective-permute-start.15
  478.3 2.4 collective-permute-start.14
  480.8 3.1 collective-permute-start.13
  483.9 1.9 collective-permute-start.12
  485.9 2.9 collective-permute-done.13
  488.8 2.5 collective-permute-done.12
  494.6 51.3 %reduce-scatter.29.cloned.1.call-done = bf16[192,24]{0,1:T(8,128)(2,1)} async-done(((bf16[192,768]{0,1:T(8,128)(2,1)}), bf16[192,24]{0,1:T(8,128)(2,1)}) %reduce-scatter.29.cloned.1.call-update) | async-done | bytes 9232 | tf_op jit(solution)/shard_map/reduce_scatter | solution.py:241
  545.9 121.3 %reduce-scatter.27.cloned.1.call-done = bf16[192,24]{0,1:T(8,128)(2,1)} async-done(((bf16[192,768]{0,1:T(8,128)(2,1)}), bf16[192,24]{0,1:T(8,128)(2,1)}) %reduce-scatter.27.cloned.1.call-update) | async-done | bytes 9232 | tf_op jit(solution)/shard_map/reduce_scatter | solution.py:241
  667.2 64.4 %all-reduce.19 = (bf16[192,18]{0,1:T(8,128)(2,1)S(1)}, bf16[192,18]{0,1:T(8,128)(2,1)S(1)}, bf16[192,6]{0,1:T(8,128)(2,1)S(1)}, bf16[192,6]{0,1:T(8,128)(2,1)S(1...) all-reduce(bf16[192,18]{0,1:T(8,128)(2,1)S(1)} %constant_dynamic-sl, ...), channel_id=5, replica_groups=mesh['rows'=16,'cols'=32] {'rows'}, use_global_device_ids=true, to_apply=%region_25.26.clone | all-reduce | flops 18432 | bytes 73728
  (416 shorter events, 110.7 us)
Async XLA Ops:
  7.2 485.2 %reduce-scatter.31.cloned.1.call-start = ((), (), s32[]{:S(2)}) async-start(), calls=%async_computation.6 | async-start | bytes 208896
  8.5 33.5 %collective-permute-start.4 = (bf16[4,32]{1,0:T(4,128)(2,1)}, bf16[4,32]{1,0:T(4,128)(2,1)}, u32[]{:S(2)}, u32[]{:S(2)}) collective-permute-start(bf16[4,32]{1,0:T(4,128)(2,1)} %get-tuple-element.76), channel_id=1, source_target_pairs={{0,32},{32,64},{64,96},{96,128},{128,160},{160,192},{192,224},{224... | collective-permute-start | bytes 776 | tf_op jit(solution)/shard_map/ppermute | solution.py:20
  13.4 28.6 %collective-permute-start.5 = (bf16[4,32]{1,0:T(4,128)(2,1)}, bf16[4,32]{1,0:T(4,128)(2,1)}, u32[]{:S(2)}, u32[]{:S(2)}) collective-permute-start(bf16[4,32]{1,0:T(4,128)(2,1)} %get-tuple-element.77), channel_id=1, source_target_pairs={{32,0},{64,32},{96,64},{128,96},{160,128},{192,160},{224,192},{256... | collective-permute-start | bytes 776 | tf_op jit(solution)/shard_map/ppermute | solution.py:23
  31.9 20.6 %collective-permute-start.1 = (bf16[4,32,192]{2,1,0:T(8,128)(2,1)S(1)}, bf16[4,32,192]{2,1,0:T(8,128)(2,1)S(1)}, u32[]{:S(2)}, u32[]{:S(2)}) collective-permute-start(bf16[4,32,192]{2,1,0:T(8,128)(2,1)S(1)} %bitcast.340), channel_id=1, source_target_pairs={{32,0},{64,32},{96,64},{128,96},{160,128},{192,160},{224,192},{256... | collective-permute-start | bytes 147464 | tf_op jit(solution)/shard_map/ppermute | solution.py:23
  33.3 19.3 %collective-permute-start = (bf16[4,32,192]{2,1,0:T(8,128)(2,1)S(1)}, bf16[4,32,192]{2,1,0:T(8,128)(2,1)S(1)}, u32[]{:S(2)}, u32[]{:S(2)}) collective-permute-start(bf16[4,32,192]{2,1,0:T(8,128)(2,1)S(1)} %bitcast.341), channel_id=1, source_target_pairs={{0,32},{32,64},{64,96},{96,128},{128,160},{160,192},{192,224},{224... | collective-permute-start | bytes 147464 | tf_op jit(solution)/shard_map/ppermute | solution.py:20
  42.8 8.8 %collective-permute-start.6 = (bf16[16,4]{1,0:T(8,128)(2,1)S(1)}, bf16[16,4]{1,0:T(8,128)(2,1)S(1)}, u32[]{:S(2)}, u32[]{:S(2)}) collective-permute-start(bf16[16,4]{1,0:T(8,128)(2,1)S(1)} %get-tuple-element.74), channel_id=1, source_target_pairs={{0,1},{1,2},{2,3},{3,4},{4,5},{5,6},{6,7},{7,8},{8,9},{9,10},{10,1... | collective-permute-start | bytes 392 | tf_op jit(solution)/shard_map/ppermute | solution.py:20
  44.7 7.4 collective-permute-start.7
  52.6 8.8 %collective-permute-start.2 = (bf16[16,4,192]{2,1,0:T(4,128)(2,1)S(1)}, bf16[16,4,192]{2,1,0:T(4,128)(2,1)S(1)}, u32[]{:S(2)}, u32[]{:S(2)}) collective-permute-start(bf16[16,4,192]{2,1,0:T(4,128)(2,1)S(1)} %get-tuple-element.66), channel_id=1, source_target_pairs={{0,1},{1,2},{2,3},{3,4},{4,5},{5,6},{6,7},{7,8},{8,9},{9,10},{10,1... | collective-permute-start | bytes 73736 | tf_op jit(solution)/shard_map/ppermute | solution.py:20
  56.7 5.4 collective-permute-start.3
  115.4 8.8 %collective-permute-start.8 = (bf16[16,4,192]{2,1,0:T(4,128)(2,1)S(1)}, bf16[16,4,192]{2,1,0:T(4,128)(2,1)S(1)}, u32[]{:S(2)}, u32[]{:S(2)}) collective-permute-start(bf16[16,4,192]{2,1,0:T(4,128)(2,1)S(1)} %get-tuple-element.62), channel_id=1, source_target_pairs={{0,1},{1,2},{2,3},{3,4},{4,5},{5,6},{6,7},{7,8},{8,9},{9,10},{10,1... | collective-permute-start | bytes 73736 | tf_op jit(solution)/shard_map/ppermute | solution.py:20
  118.7 6.3 collective-permute-start.9
  125.2 6.9 collective-permute-start.10
  129.9 8.1 %collective-permute-start.11 = (bf16[4,32,192]{2,1,0:T(8,128)(2,1)S(1)}, bf16[4,32,192]{2,1,0:T(8,128)(2,1)S(1)}, u32[]{:S(2)}, u32[]{:S(2)}) collective-permute-start(bf16[4,32,192]{2,1,0:T(8,128)(2,1)S(1)} %get-tuple-element.65), channel_id=1, source_target_pairs={{32,0},{64,32},{96,64},{128,96},{160,128},{192,160},{224,192},{256... | collective-permute-start | bytes 147464 | tf_op jit(solution)/shard_map/ppermute | solution.py:23
  214.8 28.2 %collective-permute-start.51 = (bf16[768,6]{0,1:T(8,128)(2,1)S(1)}, bf16[768,6]{0,1:T(8,128)(2,1)S(1)}, u32[]{:S(2)}, u32[]{:S(2)}) collective-permute-start(bf16[768,6]{0,1:T(8,128)(2,1)S(1)} %slice.212), channel_id=1, source_target_pairs={{0,8},{1,9},{2,10},{3,11},{4,12},{5,13},{6,14},{7,15},{8,16},{9,17... | collective-permute-start | bytes 27656
  235.2 16.9 %collective-permute-start.50 = (bf16[768,8]{0,1:T(8,128)(2,1)S(1)}, bf16[768,8]{0,1:T(8,128)(2,1)S(1)}, u32[]{:S(2)}, u32[]{:S(2)}) collective-permute-start(bf16[768,8]{0,1:T(8,128)(2,1)S(1)} %get-tuple-element.41), channel_id=1, source_target_pairs={{0,7},{1,8},{2,9},{3,10},{4,11},{5,12},{6,13},{7,14},{8,15},{9,16}... | collective-permute-start | bytes 36872
  237.2 16.9 %collective-permute-start.49 = (bf16[768,8]{0,1:T(8,128)(2,1)S(1)}, bf16[768,8]{0,1:T(8,128)(2,1)S(1)}, u32[]{:S(2)}, u32[]{:S(2)}) collective-permute-start(bf16[768,8]{0,1:T(8,128)(2,1)S(1)} %get-tuple-element.41), channel_id=1, source_target_pairs={{0,6},{1,7},{2,8},{3,9},{4,10},{5,11},{6,12},{7,13},{8,14},{9,15},... | collective-permute-start | bytes 36872
  239.1 16.9 %collective-permute-start.48 = (bf16[768,8]{0,1:T(8,128)(2,1)S(1)}, bf16[768,8]{0,1:T(8,128)(2,1)S(1)}, u32[]{:S(2)}, u32[]{:S(2)}) collective-permute-start(bf16[768,8]{0,1:T(8,128)(2,1)S(1)} %get-tuple-element.41), channel_id=1, source_target_pairs={{0,5},{1,6},{2,7},{3,8},{4,9},{5,10},{6,11},{7,12},{8,13},{9,14},{... | collective-permute-start | bytes 36872
  241.0 17.2 %collective-permute-start.47 = (bf16[768,8]{0,1:T(8,128)(2,1)S(1)}, bf16[768,8]{0,1:T(8,128)(2,1)S(1)}, u32[]{:S(2)}, u32[]{:S(2)}) collective-permute-start(bf16[768,8]{0,1:T(8,128)(2,1)S(1)} %get-tuple-element.41), channel_id=1, source_target_pairs={{0,4},{1,5},{2,6},{3,7},{4,8},{5,9},{6,10},{7,11},{8,12},{9,13},{1... | collective-permute-start | bytes 36872
  243.0 17.2 %collective-permute-start.46 = (bf16[768,8]{0,1:T(8,128)(2,1)S(1)}, bf16[768,8]{0,1:T(8,128)(2,1)S(1)}, u32[]{:S(2)}, u32[]{:S(2)}) collective-permute-start(bf16[768,8]{0,1:T(8,128)(2,1)S(1)} %get-tuple-element.41), channel_id=1, source_target_pairs={{0,3},{1,4},{2,5},{3,6},{4,7},{5,8},{6,9},{7,10},{8,11},{9,12},{10... | collective-permute-start | bytes 36872
  252.1 19.8 %collective-permute-start.58 = (bf16[768,8]{0,1:T(8,128)(2,1)S(1)}, bf16[768,8]{0,1:T(8,128)(2,1)S(1)}, u32[]{:S(2)}, u32[]{:S(2)}) collective-permute-start(bf16[768,8]{0,1:T(8,128)(2,1)S(1)} %get-tuple-element.40), channel_id=1, source_target_pairs={{0,7},{1,8},{2,9},{3,10},{4,11},{5,12},{6,13},{7,14},{8,15},{9,16}... | collective-permute-start | bytes 36872
  254.0 21.2 %collective-permute-start.57 = (bf16[768,8]{0,1:T(8,128)(2,1)S(1)}, bf16[768,8]{0,1:T(8,128)(2,1)S(1)}, u32[]{:S(2)}, u32[]{:S(2)}) collective-permute-start(bf16[768,8]{0,1:T(8,128)(2,1)S(1)} %get-tuple-element.40), channel_id=1, source_target_pairs={{0,6},{1,7},{2,8},{3,9},{4,10},{5,11},{6,12},{7,13},{8,14},{9,15},... | collective-permute-start | bytes 36872
  256.0 8.0 %collective-permute-start.45 = (bf16[768,8]{0,1:T(8,128)(2,1)S(1)}, bf16[768,8]{0,1:T(8,128)(2,1)S(1)}, u32[]{:S(2)}, u32[]{:S(2)}) collective-permute-start(bf16[768,8]{0,1:T(8,128)(2,1)S(1)} %get-tuple-element.41), channel_id=1, source_target_pairs={{0,2},{1,3},{2,4},{3,5},{4,6},{5,7},{6,8},{7,9},{8,10},{9,11},{10,... | collective-permute-start | bytes 36872
  258.2 7.7 %collective-permute-start.44 = (bf16[768,8]{0,1:T(8,128)(2,1)S(1)}, bf16[768,8]{0,1:T(8,128)(2,1)S(1)}, u32[]{:S(2)}, u32[]{:S(2)}) collective-permute-start(bf16[768,8]{0,1:T(8,128)(2,1)S(1)} %get-tuple-element.41), channel_id=1, source_target_pairs={{0,1},{1,2},{2,3},{3,4},{4,5},{5,6},{6,7},{7,8},{8,9},{9,10},{10,1... | collective-permute-start | bytes 36872
  260.1 8.6 %collective-permute-start.59 = (bf16[768,6]{0,1:T(8,128)(2,1)S(1)}, bf16[768,6]{0,1:T(8,128)(2,1)S(1)}, u32[]{:S(2)}, u32[]{:S(2)}) collective-permute-start(bf16[768,6]{0,1:T(8,128)(2,1)S(1)} %slice.213), channel_id=1, source_target_pairs={{0,8},{1,9},{2,10},{3,11},{4,12},{5,13},{6,14},{7,15},{8,16},{9,17... | collective-permute-start | bytes 27656
  264.0 14.2 %collective-permute-start.56 = (bf16[768,8]{0,1:T(8,128)(2,1)S(1)}, bf16[768,8]{0,1:T(8,128)(2,1)S(1)}, u32[]{:S(2)}, u32[]{:S(2)}) collective-permute-start(bf16[768,8]{0,1:T(8,128)(2,1)S(1)} %get-tuple-element.40), channel_id=1, source_target_pairs={{0,5},{1,6},{2,7},{3,8},{4,9},{5,10},{6,11},{7,12},{8,13},{9,14},{... | collective-permute-start | bytes 36872
  265.9 12.2 %collective-permute-start.55 = (bf16[768,8]{0,1:T(8,128)(2,1)S(1)}, bf16[768,8]{0,1:T(8,128)(2,1)S(1)}, u32[]{:S(2)}, u32[]{:S(2)}) collective-permute-start(bf16[768,8]{0,1:T(8,128)(2,1)S(1)} %get-tuple-element.40), channel_id=1, source_target_pairs={{0,4},{1,5},{2,6},{3,7},{4,8},{5,9},{6,10},{7,11},{8,12},{9,13},{1... | collective-permute-start | bytes 36872
  268.8 9.4 %collective-permute-start.54 = (bf16[768,8]{0,1:T(8,128)(2,1)S(1)}, bf16[768,8]{0,1:T(8,128)(2,1)S(1)}, u32[]{:S(2)}, u32[]{:S(2)}) collective-permute-start(bf16[768,8]{0,1:T(8,128)(2,1)S(1)} %get-tuple-element.40), channel_id=1, source_target_pairs={{0,3},{1,4},{2,5},{3,6},{4,7},{5,8},{6,9},{7,10},{8,11},{9,12},{10... | collective-permute-start | bytes 36872
  271.9 8.0 %collective-permute-start.53 = (bf16[768,8]{0,1:T(8,128)(2,1)S(1)}, bf16[768,8]{0,1:T(8,128)(2,1)S(1)}, u32[]{:S(2)}, u32[]{:S(2)}) collective-permute-start(bf16[768,8]{0,1:T(8,128)(2,1)S(1)} %get-tuple-element.40), channel_id=1, source_target_pairs={{0,2},{1,3},{2,4},{3,5},{4,6},{5,7},{6,8},{7,9},{8,10},{9,11},{10,... | collective-permute-start | bytes 36872
  275.3 7.4 %collective-permute-start.52 = (bf16[768,8]{0,1:T(8,128)(2,1)S(1)}, bf16[768,8]{0,1:T(8,128)(2,1)S(1)}, u32[]{:S(2)}, u32[]{:S(2)}) collective-permute-start(bf16[768,8]{0,1:T(8,128)(2,1)S(1)} %get-tuple-element.40), channel_id=1, source_target_pairs={{0,1},{1,2},{2,3},{3,4},{4,5},{5,6},{6,7},{7,8},{8,9},{9,10},{10,1... | collective-permute-start | bytes 36872
  278.1 215.1 %reduce-scatter.33.cloned.1.call-start = ((), (), s32[]{:S(2)}) async-start(), calls=%async_computation.7 | async-start | bytes 208896
  284.5 261.4 %reduce-scatter.29.cloned.1.call-start = ((), (), s32[]{:S(2)}) async-start(), calls=%async_computation.5 | async-start | bytes 405504 | tf_op jit(solution)/shard_map/reduce_scatter | solution.py:241
  286.2 381.0 %reduce-scatter.27.cloned.1.call-start = ((), (), s32[]{:S(2)}) async-start(), calls=%async_computation.4 | async-start | bytes 405504 | tf_op jit(solution)/shard_map/reduce_scatter | solution.py:241
  287.5 21.5 %collective-permute-start.42 = (bf16[192,8]{0,1:T(8,128)(2,1)S(1)}, bf16[192,8]{0,1:T(8,128)(2,1)S(1)}, u32[]{:S(2)}, u32[]{:S(2)}) collective-permute-start(bf16[192,8]{0,1:T(8,128)(2,1)S(1)} %get-tuple-element.38), channel_id=1, source_target_pairs={{0,7},{1,8},{2,9},{3,10},{4,11},{5,12},{6,13},{7,14},{8,15},{9,16}... | collective-permute-start | bytes 9224
  289.5 21.6 %collective-permute-start.41 = (bf16[192,8]{0,1:T(8,128)(2,1)S(1)}, bf16[192,8]{0,1:T(8,128)(2,1)S(1)}, u32[]{:S(2)}, u32[]{:S(2)}) collective-permute-start(bf16[192,8]{0,1:T(8,128)(2,1)S(1)} %get-tuple-element.38), channel_id=1, source_target_pairs={{0,6},{1,7},{2,8},{3,9},{4,10},{5,11},{6,12},{7,13},{8,14},{9,15},... | collective-permute-start | bytes 9224
  291.4 21.8 %collective-permute-start.40 = (bf16[192,8]{0,1:T(8,128)(2,1)S(1)}, bf16[192,8]{0,1:T(8,128)(2,1)S(1)}, u32[]{:S(2)}, u32[]{:S(2)}) collective-permute-start(bf16[192,8]{0,1:T(8,128)(2,1)S(1)} %get-tuple-element.38), channel_id=1, source_target_pairs={{0,5},{1,6},{2,7},{3,8},{4,9},{5,10},{6,11},{7,12},{8,13},{9,14},{... | collective-permute-start | bytes 9224
  294.5 7.8 %collective-permute-start.35 = (bf16[192,6]{0,1:T(8,128)(2,1)S(1)}, bf16[192,6]{0,1:T(8,128)(2,1)S(1)}, u32[]{:S(2)}, u32[]{:S(2)}) collective-permute-start(bf16[192,6]{0,1:T(8,128)(2,1)S(1)} %slice.210), channel_id=1, source_target_pairs={{0,8},{1,9},{2,10},{3,11},{4,12},{5,13},{6,14},{7,15},{8,16},{9,17... | collective-permute-start | bytes 6920
  296.4 7.8 %collective-permute-start.43 = (bf16[192,6]{0,1:T(8,128)(2,1)S(1)}, bf16[192,6]{0,1:T(8,128)(2,1)S(1)}, u32[]{:S(2)}, u32[]{:S(2)}) collective-permute-start(bf16[192,6]{0,1:T(8,128)(2,1)S(1)} %slice.211), channel_id=1, source_target_pairs={{0,8},{1,9},{2,10},{3,11},{4,12},{5,13},{6,14},{7,15},{8,16},{9,17... | collective-permute-start | bytes 6920
  302.3 15.1 %collective-permute-start.39 = (bf16[192,8]{0,1:T(8,128)(2,1)S(1)}, bf16[192,8]{0,1:T(8,128)(2,1)S(1)}, u32[]{:S(2)}, u32[]{:S(2)}) collective-permute-start(bf16[192,8]{0,1:T(8,128)(2,1)S(1)} %get-tuple-element.38), channel_id=1, source_target_pairs={{0,4},{1,5},{2,6},{3,7},{4,8},{5,9},{6,10},{7,11},{8,12},{9,13},{1... | collective-permute-start | bytes 9224
  304.3 15.1 %collective-permute-start.38 = (bf16[192,8]{0,1:T(8,128)(2,1)S(1)}, bf16[192,8]{0,1:T(8,128)(2,1)S(1)}, u32[]{:S(2)}, u32[]{:S(2)}) collective-permute-start(bf16[192,8]{0,1:T(8,128)(2,1)S(1)} %get-tuple-element.38), channel_id=1, source_target_pairs={{0,3},{1,4},{2,5},{3,6},{4,7},{5,8},{6,9},{7,10},{8,11},{9,12},{10... | collective-permute-start | bytes 9224
  308.9 117.0 %collective-permute-start.37 = (bf16[192,8]{0,1:T(8,128)(2,1)S(1)}, bf16[192,8]{0,1:T(8,128)(2,1)S(1)}, u32[]{:S(2)}, u32[]{:S(2)}) collective-permute-start(bf16[192,8]{0,1:T(8,128)(2,1)S(1)} %get-tuple-element.38), channel_id=1, source_target_pairs={{0,2},{1,3},{2,4},{3,5},{4,6},{5,7},{6,8},{7,9},{8,10},{9,11},{10,... | collective-permute-start | bytes 9224
  311.1 118.1 %collective-permute-start.36 = (bf16[192,8]{0,1:T(8,128)(2,1)S(1)}, bf16[192,8]{0,1:T(8,128)(2,1)S(1)}, u32[]{:S(2)}, u32[]{:S(2)}) collective-permute-start(bf16[192,8]{0,1:T(8,128)(2,1)S(1)} %get-tuple-element.38), channel_id=1, source_target_pairs={{0,1},{1,2},{2,3},{3,4},{4,5},{5,6},{6,7},{7,8},{8,9},{9,10},{10,1... | collective-permute-start | bytes 9224
  313.2 117.9 %collective-permute-start.34 = (bf16[192,8]{0,1:T(8,128)(2,1)S(1)}, bf16[192,8]{0,1:T(8,128)(2,1)S(1)}, u32[]{:S(2)}, u32[]{:S(2)}) collective-permute-start(bf16[192,8]{0,1:T(8,128)(2,1)S(1)} %get-tuple-element.39), channel_id=1, source_target_pairs={{0,7},{1,8},{2,9},{3,10},{4,11},{5,12},{6,13},{7,14},{8,15},{9,16}... | collective-permute-start | bytes 9224
  317.5 118.5 %collective-permute-start.33 = (bf16[192,8]{0,1:T(8,128)(2,1)S(1)}, bf16[192,8]{0,1:T(8,128)(2,1)S(1)}, u32[]{:S(2)}, u32[]{:S(2)}) collective-permute-start(bf16[192,8]{0,1:T(8,128)(2,1)S(1)} %get-tuple-element.39), channel_id=1, source_target_pairs={{0,6},{1,7},{2,8},{3,9},{4,10},{5,11},{6,12},{7,13},{8,14},{9,15},... | collective-permute-start | bytes 9224
  319.4 118.5 %collective-permute-start.32 = (bf16[192,8]{0,1:T(8,128)(2,1)S(1)}, bf16[192,8]{0,1:T(8,128)(2,1)S(1)}, u32[]{:S(2)}, u32[]{:S(2)}) collective-permute-start(bf16[192,8]{0,1:T(8,128)(2,1)S(1)} %get-tuple-element.39), channel_id=1, source_target_pairs={{0,5},{1,6},{2,7},{3,8},{4,9},{5,10},{6,11},{7,12},{8,13},{9,14},{... | collective-permute-start | bytes 9224
  426.0 17.8 %collective-permute-start.31 = (bf16[192,8]{0,1:T(8,128)(2,1)S(1)}, bf16[192,8]{0,1:T(8,128)(2,1)S(1)}, u32[]{:S(2)}, u32[]{:S(2)}) collective-permute-start(bf16[192,8]{0,1:T(8,128)(2,1)S(1)} %get-tuple-element.39), channel_id=1, source_target_pairs={{0,4},{1,5},{2,6},{3,7},{4,8},{5,9},{6,10},{7,11},{8,12},{9,13},{1... | collective-permute-start | bytes 9224
  429.2 20.1 %collective-permute-start.30 = (bf16[192,8]{0,1:T(8,128)(2,1)S(1)}, bf16[192,8]{0,1:T(8,128)(2,1)S(1)}, u32[]{:S(2)}, u32[]{:S(2)}) collective-permute-start(bf16[192,8]{0,1:T(8,128)(2,1)S(1)} %get-tuple-element.39), channel_id=1, source_target_pairs={{0,3},{1,4},{2,5},{3,6},{4,7},{5,8},{6,9},{7,10},{8,11},{9,12},{10... | collective-permute-start | bytes 9224
  431.1 22.2 %collective-permute-start.29 = (bf16[192,8]{0,1:T(8,128)(2,1)S(1)}, bf16[192,8]{0,1:T(8,128)(2,1)S(1)}, u32[]{:S(2)}, u32[]{:S(2)}) collective-permute-start(bf16[192,8]{0,1:T(8,128)(2,1)S(1)} %get-tuple-element.39), channel_id=1, source_target_pairs={{0,2},{1,3},{2,4},{3,5},{4,6},{5,7},{6,8},{7,9},{8,10},{9,11},{10,... | collective-permute-start | bytes 9224
  435.9 19.3 %collective-permute-start.28 = (bf16[192,8]{0,1:T(8,128)(2,1)S(1)}, bf16[192,8]{0,1:T(8,128)(2,1)S(1)}, u32[]{:S(2)}, u32[]{:S(2)}) collective-permute-start(bf16[192,8]{0,1:T(8,128)(2,1)S(1)} %get-tuple-element.39), channel_id=1, source_target_pairs={{0,1},{1,2},{2,3},{3,4},{4,5},{5,6},{6,7},{7,8},{8,9},{9,10},{10,1... | collective-permute-start | bytes 9224
  437.9 19.3 %collective-permute-start.27 = (bf16[192,18]{0,1:T(8,128)(2,1)S(1)}, bf16[192,18]{0,1:T(8,128)(2,1)S(1)}, u32[]{:S(2)}, u32[]{:S(2)}) collective-permute-start(bf16[192,18]{0,1:T(8,128)(2,1)S(1)} %slice.209), channel_id=1, source_target_pairs={{0,8},{1,9},{2,10},{3,11},{4,12},{5,13},{6,14},{7,15},{8,16},{9,17... | collective-permute-start | bytes 20744
  443.7 17.1 %collective-permute-start.26 = (bf16[192,24]{0,1:T(8,128)(2,1)S(1)}, bf16[192,24]{0,1:T(8,128)(2,1)S(1)}, u32[]{:S(2)}, u32[]{:S(2)}) collective-permute-start(bf16[192,24]{0,1:T(8,128)(2,1)S(1)} %get-tuple-element.36), channel_id=1, source_target_pairs={{0,7},{1,8},{2,9},{3,10},{4,11},{5,12},{6,13},{7,14},{8,15},{9,16}... | collective-permute-start | bytes 27656
  449.3 14.4 %collective-permute-start.25 = (bf16[192,24]{0,1:T(8,128)(2,1)S(1)}, bf16[192,24]{0,1:T(8,128)(2,1)S(1)}, u32[]{:S(2)}, u32[]{:S(2)}) collective-permute-start(bf16[192,24]{0,1:T(8,128)(2,1)S(1)} %get-tuple-element.36), channel_id=1, source_target_pairs={{0,6},{1,7},{2,8},{3,9},{4,10},{5,11},{6,12},{7,13},{8,14},{9,15},... | collective-permute-start | bytes 27656
  453.3 12.3 %collective-permute-start.24 = (bf16[192,24]{0,1:T(8,128)(2,1)S(1)}, bf16[192,24]{0,1:T(8,128)(2,1)S(1)}, u32[]{:S(2)}, u32[]{:S(2)}) collective-permute-start(bf16[192,24]{0,1:T(8,128)(2,1)S(1)} %get-tuple-element.36), channel_id=1, source_target_pairs={{0,5},{1,6},{2,7},{3,8},{4,9},{5,10},{6,11},{7,12},{8,13},{9,14},{... | collective-permute-start | bytes 27656
  455.2 13.7 %collective-permute-start.23 = (bf16[192,24]{0,1:T(8,128)(2,1)S(1)}, bf16[192,24]{0,1:T(8,128)(2,1)S(1)}, u32[]{:S(2)}, u32[]{:S(2)}) collective-permute-start(bf16[192,24]{0,1:T(8,128)(2,1)S(1)} %get-tuple-element.36), channel_id=1, source_target_pairs={{0,4},{1,5},{2,6},{3,7},{4,8},{5,9},{6,10},{7,11},{8,12},{9,13},{1... | collective-permute-start | bytes 27656
  457.2 13.7 %collective-permute-start.22 = (bf16[192,24]{0,1:T(8,128)(2,1)S(1)}, bf16[192,24]{0,1:T(8,128)(2,1)S(1)}, u32[]{:S(2)}, u32[]{:S(2)}) collective-permute-start(bf16[192,24]{0,1:T(8,128)(2,1)S(1)} %get-tuple-element.36), channel_id=1, source_target_pairs={{0,3},{1,4},{2,5},{3,6},{4,7},{5,8},{6,9},{7,10},{8,11},{9,12},{10... | collective-permute-start | bytes 27656
  460.9 12.0 %collective-permute-start.21 = (bf16[192,24]{0,1:T(8,128)(2,1)S(1)}, bf16[192,24]{0,1:T(8,128)(2,1)S(1)}, u32[]{:S(2)}, u32[]{:S(2)}) collective-permute-start(bf16[192,24]{0,1:T(8,128)(2,1)S(1)} %get-tuple-element.36), channel_id=1, source_target_pairs={{0,2},{1,3},{2,4},{3,5},{4,6},{5,7},{6,8},{7,9},{8,10},{9,11},{10,... | collective-permute-start | bytes 27656
  463.7 11.1 %collective-permute-start.20 = (bf16[192,24]{0,1:T(8,128)(2,1)S(1)}, bf16[192,24]{0,1:T(8,128)(2,1)S(1)}, u32[]{:S(2)}, u32[]{:S(2)}) collective-permute-start(bf16[192,24]{0,1:T(8,128)(2,1)S(1)} %get-tuple-element.36), channel_id=1, source_target_pairs={{0,1},{1,2},{2,3},{3,4},{4,5},{5,6},{6,7},{7,8},{8,9},{9,10},{10,1... | collective-permute-start | bytes 27656
  465.6 15.1 %collective-permute-start.18 = (bf16[192,24]{0,1:T(8,128)(2,1)S(1)}, bf16[192,24]{0,1:T(8,128)(2,1)S(1)}, u32[]{:S(2)}, u32[]{:S(2)}) collective-permute-start(bf16[192,24]{0,1:T(8,128)(2,1)S(1)} %get-tuple-element.37), channel_id=1, source_target_pairs={{0,7},{1,8},{2,9},{3,10},{4,11},{5,12},{6,13},{7,14},{8,15},{9,16}... | collective-permute-start | bytes 27656
  469.0 14.9 %collective-permute-start.17 = (bf16[192,24]{0,1:T(8,128)(2,1)S(1)}, bf16[192,24]{0,1:T(8,128)(2,1)S(1)}, u32[]{:S(2)}, u32[]{:S(2)}) collective-permute-start(bf16[192,24]{0,1:T(8,128)(2,1)S(1)} %get-tuple-element.37), channel_id=1, source_target_pairs={{0,6},{1,7},{2,8},{3,9},{4,10},{5,11},{6,12},{7,13},{8,14},{9,15},... | collective-permute-start | bytes 27656
  470.9 7.4 %collective-permute-start.19 = (bf16[192,18]{0,1:T(8,128)(2,1)S(1)}, bf16[192,18]{0,1:T(8,128)(2,1)S(1)}, u32[]{:S(2)}, u32[]{:S(2)}) collective-permute-start(bf16[192,18]{0,1:T(8,128)(2,1)S(1)} %slice.208), channel_id=1, source_target_pairs={{0,8},{1,9},{2,10},{3,11},{4,12},{5,13},{6,14},{7,15},{8,16},{9,17... | collective-permute-start | bytes 20744
  472.9 12.9 %collective-permute-start.16 = (bf16[192,24]{0,1:T(8,128)(2,1)S(1)}, bf16[192,24]{0,1:T(8,128)(2,1)S(1)}, u32[]{:S(2)}, u32[]{:S(2)}) collective-permute-start(bf16[192,24]{0,1:T(8,128)(2,1)S(1)} %get-tuple-element.37), channel_id=1, source_target_pairs={{0,5},{1,6},{2,7},{3,8},{4,9},{5,10},{6,11},{7,12},{8,13},{9,14},{... | collective-permute-start | bytes 27656
  474.8 11.0 %collective-permute-start.15 = (bf16[192,24]{0,1:T(8,128)(2,1)S(1)}, bf16[192,24]{0,1:T(8,128)(2,1)S(1)}, u32[]{:S(2)}, u32[]{:S(2)}) collective-permute-start(bf16[192,24]{0,1:T(8,128)(2,1)S(1)} %get-tuple-element.37), channel_id=1, source_target_pairs={{0,4},{1,5},{2,6},{3,7},{4,8},{5,9},{6,10},{7,11},{8,12},{9,13},{1... | collective-permute-start | bytes 27656
  478.3 7.5 %collective-permute-start.14 = (bf16[192,24]{0,1:T(8,128)(2,1)S(1)}, bf16[192,24]{0,1:T(8,128)(2,1)S(1)}, u32[]{:S(2)}, u32[]{:S(2)}) collective-permute-start(bf16[192,24]{0,1:T(8,128)(2,1)S(1)} %get-tuple-element.37), channel_id=1, source_target_pairs={{0,3},{1,4},{2,5},{3,6},{4,7},{5,8},{6,9},{7,10},{8,11},{9,12},{10... | collective-permute-start | bytes 27656
  480.8 8.0 %collective-permute-start.13 = (bf16[192,24]{0,1:T(8,128)(2,1)S(1)}, bf16[192,24]{0,1:T(8,128)(2,1)S(1)}, u32[]{:S(2)}, u32[]{:S(2)}) collective-permute-start(bf16[192,24]{0,1:T(8,128)(2,1)S(1)} %get-tuple-element.37), channel_id=1, source_target_pairs={{0,2},{1,3},{2,4},{3,5},{4,6},{5,7},{6,8},{7,9},{8,10},{9,11},{10,... | collective-permute-start | bytes 27656
  483.9 7.4 %collective-permute-start.12 = (bf16[192,24]{0,1:T(8,128)(2,1)S(1)}, bf16[192,24]{0,1:T(8,128)(2,1)S(1)}, u32[]{:S(2)}, u32[]{:S(2)}) collective-permute-start(bf16[192,24]{0,1:T(8,128)(2,1)S(1)} %get-tuple-element.37), channel_id=1, source_target_pairs={{0,1},{1,2},{2,3},{3,4},{4,5},{5,6},{6,7},{7,8},{8,9},{9,10},{10,1... | collective-permute-start | bytes 27656
  (72 other events, 912.1 us)
Sparse Core Ops, SparseCore 0:
  278.2 76.3 reduce-scatter.30
  357.3 69.7 reduce-scatter.32
  431.8 114.0 reduce-scatter.28
  550.3 116.8 reduce-scatter.26
where the time goes:
time: 751 us; the launch traced here: 741 us
  blocking collectives  237 us (32%)
  waiting for transfers between devices  193 us (26%)
  starting transfers between devices  182 us (24%)
  local copies, waits for them, and re-layouts  55.5 us (7%)
  matrix products  40.7 us (5%)
  between operations  18.5 us (2%)
  other arithmetic  14.1 us (2%)
    reduce_scatter x2, waiting for transfers between devices, reduce_grads(): lax.psum_scatter(inner_term.astype(jnp.bfloat16), 'cols', scatter_dimensi...  173 us
    unnamed x50, starting transfers between devices  139 us
    unnamed x2, blocking collectives  133 us
    psum x1, blocking collectives, local(): table_sum = lax.psum(jnp.stack([table_one, table_two]), ('rows', 'cols'))  105 us
    ppermute x6, starting transfers between devices, with_halo(): lax.ppermute(lax.slice_in_dim(block, block.shape[dim] - width, None, axis...  24 us
    unnamed x173, local copies, waits for them, and re-layouts  19 us
    ppermute x6, starting transfers between devices, with_halo(): lax.ppermute(lax.slice_in_dim(block, 0, width, axis=dim), axis, backward)  18.5 us
  transfers between devices with their start and end apart: 64, of which 13 were waited for; matrix products, arithmetic and copies ran while one was open for 6% of the time, Pallas kernels for 0%

commit v1 on v0

--- a/solution.py
+++ b/solution.py
@@ -376,7 +376,8 @@
         grad_mid_one.reshape(tile_rows, tile_cols, channels).astype(jnp.float32) + grad_tokens
     ).astype(jnp.bfloat16)
     summed_one = reduce_grads(qkv_one_grad, proj_one, inner_one, outer_one)
-    table_sum = lax.psum(jnp.stack([table_one, table_two]), ("rows", "cols"))
+    inner = lax.psum(jnp.stack([table_one, table_two]), "cols")
+    table_sum = lax.psum(inner, "rows")
     qkv_grad = jnp.stack([summed_one[0], summed_two[0]])
     proj_grad = jnp.stack([summed_one[1], summed_two[1]])
     inner_grad = jnp.stack([summed_one[2], summed_two[2]])

time: 751 us -> 750 us (level)
  waiting for transfers between devices: 193 us -> 111 us
  blocking collectives: 237 us -> 310 us
  starting transfers between devices: 182 us -> 191 us
    reduce_scatter x2, waiting for transfers between devices: 173 us -> 89.8 us  [reduce_grads(): lax.psum_scatter(inner_term.astype(jnp.bfloat16), 'cols', scatter_dimensi...]
    psum x1 -> x2, blocking collectives: 105 us -> 177 us  [the longest x1 114 us: local(): inner = lax.psum(jnp.stack([table_one, table_two]), 'cols')]
    unnamed x50, starting transfers between devices: 139 us -> 148 us
  transfers between devices with their start and end apart: 64 -> 64, of which waited for: 13 -> 12; matrix products, arithmetic and copies ran while one was open for 6% -> 6% of each run, Pallas kernels for 0% -> 0%
where the time goes in v1:
time: 750 us; the launch traced here: 740 us
  blocking collectives  310 us (41%)
  starting transfers between devices  191 us (25%)
  waiting for transfers between devices  111 us (15%)
  local copies, waits for them, and re-layouts  55.4 us (7%)
  matrix products  40.7 us (5%)
  between operations  18.5 us (2%)
  other arithmetic  13.5 us (2%)
    unnamed x50, starting transfers between devices  148 us
    unnamed x2, blocking collectives  133 us
    psum x1, blocking collectives, local(): inner = lax.psum(jnp.stack([table_one, table_two]), 'cols')  114 us
    reduce_scatter x2, waiting for transfers between devices, reduce_grads(): lax.psum_scatter(inner_term.astype(jnp.bfloat16), 'cols', scatter_dimensi...  89.8 us
    psum x1, blocking collectives, local(): table_sum = lax.psum(inner, 'rows')  63.8 us
    ppermute x6, starting transfers between devices, with_halo(): lax.ppermute(lax.slice_in_dim(block, block.shape[dim] - width, None, axis...  23.3 us
    unnamed x173, local copies, waits for them, and re-layouts  20.1 us
    ppermute x6, starting transfers between devices, with_halo(): lax.ppermute(lax.slice_in_dim(block, 0, width, axis=dim), axis, backward)  18.5 us
  transfers between devices with their start and end apart: 64, of which 12 were waited for; matrix products, arithmetic and copies ran while one was open for 6% of the time, Pallas kernels for 0%

profile of v1, /device:TPU:16, one launch (start us, length us, event | category | flops | bytes accessed | tf_op | source)
XLA Modules:
  0.0 739.6 jit_solution(2043835094992381282)
XLA Ops:
  8.0 4.3 collective-permute-start.4
  20.3 2.6 fusion.29
  26.2 2.9 multiply_convert_fusion.1
  31.8 5.5 collective-permute-start
  37.5 2.6 fusion.30
  42.9 6.0 collective-permute-start.7
  50.8 4.1 collective-permute-start.2
  55.0 3.9 collective-permute-start.3
  63.6 3.2 reshape.352
  68.4 2.4 fusion.136
  72.1 2.3 fusion.23
  77.4 2.8 fusion.47
  84.6 2.3 fusion.24
  90.8 2.5 copy.166
  93.3 4.1 copy.147
  97.4 5.6 convert_element_type.304
  103.0 2.6 multiply_reduce_fusion.2
  107.7 2.0 convert_element_type.320
  109.8 2.3 convolution_convert_fusion.9
  114.4 3.2 collective-permute-start.8
  117.6 4.7 collective-permute-start.9
  124.2 4.3 collective-permute-start.10
  130.6 6.0 collective-permute-done.11
  137.1 2.0 add_convert_fusion
  144.8 68.5 %fusion.122 = (bf16[192,24]{0,1:T(8,128)(2,1)S(1)}, bf16[192,24]{0,1:T(8,128)(2,1)S(1)}, bf16[192,8]{0,1:T(8,128)(2,1)S(1)}, bf16[192,8]{0,1:T(8,128)(2,1)S(1)},...) fusion(bf16[192,576]{0,1:T(8,128)(2,1)} %convolution_convert_fusion.9, ...), kind=kCustom, calls=%all-reduce-scatter.6 | all-reduce-scatter fusion | flops 786434 | bytes 1230848
  213.4 20.4 %collective-permute-start.51 = (bf16[768,6]{0,1:T(8,128)(2,1)S(1)}, bf16[768,6]{0,1:T(8,128)(2,1)S(1)}, u32[]{:S(2)}, u32[]{:S(2)}) collective-permute-start(bf16[768,6]{0,1:T(8,128)(2,1)S(1)} %slice.212), channel_id=1, source_target_pairs={{0,8},{1,9},{2,10},{3,11},{4,12},{5,13},{6,14},{7,15},{8,16},{9,17... | collective-permute-start | bytes 27656
  233.8 1.9 collective-permute-start.50
  235.7 1.9 collective-permute-start.49
  237.7 1.9 collective-permute-start.48
  241.5 4.6 collective-permute-start.46
  254.5 2.2 collective-permute-start.45
  258.7 1.9 collective-permute-start.59
  267.3 3.1 collective-permute-start.54
  270.5 3.3 collective-permute-start.53
  273.8 1.9 collective-permute-start.52
  278.5 2.8 collective-permute-done.52
  286.0 2.1 collective-permute-start.42
  293.1 1.9 collective-permute-start.35
  295.1 1.9 collective-permute-start.43
  301.0 1.9 collective-permute-start.39
  302.9 4.6 collective-permute-start.38
  307.5 113.6 %psum.14 = f32[2,225,6]{1,2,0:T(8,128)S(1)} all-reduce(f32[2,225,6]{1,2,0:T(8,128)S(1)} %pad_maximum_fusion.16), channel_id=1, replica_groups=mesh['rows'=16,'cols'=32] {'cols'}, use_global_device_ids=true, to_apply=%region_40.41 | all-reduce | flops 2700 | bytes 21600 | tf_op jit(solution)/shard_map/psum | solution.py:379
  421.1 6.8 collective-permute-start.37
  427.9 4.0 collective-permute-start.36
  431.8 15.1 %collective-permute-start.34 = (bf16[192,8]{0,1:T(8,128)(2,1)S(1)}, bf16[192,8]{0,1:T(8,128)(2,1)S(1)}, u32[]{:S(2)}, u32[]{:S(2)}) collective-permute-start(bf16[192,8]{0,1:T(8,128)(2,1)S(1)} %get-tuple-element.39), channel_id=1, source_target_pairs={{0,7},{1,8},{2,9},{3,10},{4,11},{5,12},{6,13},{7,14},{8,15},{9,16}... | collective-permute-start | bytes 9224
  447.0 2.2 collective-permute-start.33
  449.2 2.2 collective-permute-start.32
  451.4 63.8 %psum.15 = f32[2,225,6]{1,2,0:T(8,128)S(1)} all-reduce(f32[2,225,6]{1,2,0:T(8,128)S(1)} %psum.14), channel_id=1, replica_groups=mesh['rows'=16,'cols'=32] {'rows'}, use_global_device_ids=true, to_apply=%region_41.42 | all-reduce | flops 2700 | bytes 21600 | tf_op jit(solution)/shard_map/psum | solution.py:380
  517.2 1.9 collective-permute-start.30
  519.1 4.0 collective-permute-start.29
  523.2 1.9 collective-permute-start.28
  528.5 3.6 collective-permute-start.26
  532.1 1.9 collective-permute-start.25
  536.0 1.9 collective-permute-start.23
  537.9 2.9 collective-permute-start.22
  541.7 3.6 collective-permute-start.21
  545.3 1.9 collective-permute-start.20
  549.1 2.2 collective-permute-start.17
  553.3 2.2 collective-permute-start.16
  561.8 3.6 collective-permute-start.13
  567.4 2.4 collective-permute-done.13
  569.8 3.0 collective-permute-done.12
  576.2 89.8 %reduce-scatter.27.cloned.1.call-done = bf16[192,24]{0,1:T(8,128)(2,1)} async-done(((bf16[192,768]{0,1:T(8,128)(2,1)}), bf16[192,24]{0,1:T(8,128)(2,1)}) %reduce-scatter.27.cloned.1.call-update) | async-done | bytes 9232 | tf_op jit(solution)/shard_map/reduce_scatter | solution.py:241
  666.0 64.4 %all-reduce.19 = (bf16[192,18]{0,1:T(8,128)(2,1)S(1)}, bf16[192,18]{0,1:T(8,128)(2,1)S(1)}, bf16[192,6]{0,1:T(8,128)(2,1)S(1)}, bf16[192,6]{0,1:T(8,128)(2,1)S(1...) all-reduce(bf16[192,18]{0,1:T(8,128)(2,1)S(1)} %constant_dynamic-sl, ...), channel_id=5, replica_groups=mesh['rows'=16,'cols'=32] {'rows'}, use_global_device_ids=true, to_apply=%region_25.26.clone | all-reduce | flops 18432 | bytes 73728
  (417 shorter events, 110.8 us)
Async XLA Ops:
  7.2 566.8 %reduce-scatter.31.cloned.1.call-start = ((), (), s32[]{:S(2)}) async-start(), calls=%async_computation.6 | async-start | bytes 208896
  8.0 32.9 %collective-permute-start.4 = (bf16[4,32]{1,0:T(4,128)(2,1)S(1)}, bf16[4,32]{1,0:T(4,128)(2,1)S(1)}, u32[]{:S(2)}, u32[]{:S(2)}) collective-permute-start(bf16[4,32]{1,0:T(4,128)(2,1)S(1)} %get-tuple-element.76), channel_id=1, source_target_pairs={{0,32},{32,64},{64,96},{96,128},{128,160},{160,192},{192,224},{224... | collective-permute-start | bytes 776 | tf_op jit(solution)/shard_map/ppermute | solution.py:20
  12.2 28.6 %collective-permute-start.5 = (bf16[4,32]{1,0:T(4,128)(2,1)S(1)}, bf16[4,32]{1,0:T(4,128)(2,1)S(1)}, u32[]{:S(2)}, u32[]{:S(2)}) collective-permute-start(bf16[4,32]{1,0:T(4,128)(2,1)S(1)} %get-tuple-element.77), channel_id=1, source_target_pairs={{32,0},{64,32},{96,64},{128,96},{160,128},{192,160},{224,192},{256... | collective-permute-start | bytes 776 | tf_op jit(solution)/shard_map/ppermute | solution.py:23
  30.4 20.3 %collective-permute-start.1 = (bf16[4,32,192]{2,1,0:T(8,128)(2,1)S(1)}, bf16[4,32,192]{2,1,0:T(8,128)(2,1)S(1)}, u32[]{:S(2)}, u32[]{:S(2)}) collective-permute-start(bf16[4,32,192]{2,1,0:T(8,128)(2,1)S(1)} %bitcast.340), channel_id=1, source_target_pairs={{32,0},{64,32},{96,64},{128,96},{160,128},{192,160},{224,192},{256... | collective-permute-start | bytes 147464 | tf_op jit(solution)/shard_map/ppermute | solution.py:23
  31.8 18.9 %collective-permute-start = (bf16[4,32,192]{2,1,0:T(8,128)(2,1)S(1)}, bf16[4,32,192]{2,1,0:T(8,128)(2,1)S(1)}, u32[]{:S(2)}, u32[]{:S(2)}) collective-permute-start(bf16[4,32,192]{2,1,0:T(8,128)(2,1)S(1)} %bitcast.341), channel_id=1, source_target_pairs={{0,32},{32,64},{64,96},{96,128},{128,160},{160,192},{192,224},{224... | collective-permute-start | bytes 147464 | tf_op jit(solution)/shard_map/ppermute | solution.py:20
  41.0 8.8 %collective-permute-start.6 = (bf16[16,4]{1,0:T(8,128)(2,1)S(1)}, bf16[16,4]{1,0:T(8,128)(2,1)S(1)}, u32[]{:S(2)}, u32[]{:S(2)}) collective-permute-start(bf16[16,4]{1,0:T(8,128)(2,1)S(1)} %get-tuple-element.74), channel_id=1, source_target_pairs={{0,1},{1,2},{2,3},{3,4},{4,5},{5,6},{6,7},{7,8},{8,9},{9,10},{10,1... | collective-permute-start | bytes 392 | tf_op jit(solution)/shard_map/ppermute | solution.py:20
  42.9 7.4 collective-permute-start.7
  50.8 8.8 %collective-permute-start.2 = (bf16[16,4,192]{2,1,0:T(4,128)(2,1)S(1)}, bf16[16,4,192]{2,1,0:T(4,128)(2,1)S(1)}, u32[]{:S(2)}, u32[]{:S(2)}) collective-permute-start(bf16[16,4,192]{2,1,0:T(4,128)(2,1)S(1)} %get-tuple-element.66), channel_id=1, source_target_pairs={{0,1},{1,2},{2,3},{3,4},{4,5},{5,6},{6,7},{7,8},{8,9},{9,10},{10,1... | collective-permute-start | bytes 73736 | tf_op jit(solution)/shard_map/ppermute | solution.py:20
  55.0 5.4 collective-permute-start.3
  114.4 8.9 %collective-permute-start.8 = (bf16[16,4,192]{2,1,0:T(4,128)(2,1)S(1)}, bf16[16,4,192]{2,1,0:T(4,128)(2,1)S(1)}, u32[]{:S(2)}, u32[]{:S(2)}) collective-permute-start(bf16[16,4,192]{2,1,0:T(4,128)(2,1)S(1)} %get-tuple-element.62), channel_id=1, source_target_pairs={{0,1},{1,2},{2,3},{3,4},{4,5},{5,6},{6,7},{7,8},{8,9},{9,10},{10,1... | collective-permute-start | bytes 73736 | tf_op jit(solution)/shard_map/ppermute | solution.py:20
  117.6 6.3 collective-permute-start.9
  124.2 6.4 collective-permute-start.10
  128.4 8.1 %collective-permute-start.11 = (bf16[4,32,192]{2,1,0:T(8,128)(2,1)S(1)}, bf16[4,32,192]{2,1,0:T(8,128)(2,1)S(1)}, u32[]{:S(2)}, u32[]{:S(2)}) collective-permute-start(bf16[4,32,192]{2,1,0:T(8,128)(2,1)S(1)} %get-tuple-element.65), channel_id=1, source_target_pairs={{32,0},{64,32},{96,64},{128,96},{160,128},{192,160},{224,192},{256... | collective-permute-start | bytes 147464 | tf_op jit(solution)/shard_map/ppermute | solution.py:23
  213.4 28.1 %collective-permute-start.51 = (bf16[768,6]{0,1:T(8,128)(2,1)S(1)}, bf16[768,6]{0,1:T(8,128)(2,1)S(1)}, u32[]{:S(2)}, u32[]{:S(2)}) collective-permute-start(bf16[768,6]{0,1:T(8,128)(2,1)S(1)} %slice.212), channel_id=1, source_target_pairs={{0,8},{1,9},{2,10},{3,11},{4,12},{5,13},{6,14},{7,15},{8,16},{9,17... | collective-permute-start | bytes 27656
  233.8 16.9 %collective-permute-start.50 = (bf16[768,8]{0,1:T(8,128)(2,1)S(1)}, bf16[768,8]{0,1:T(8,128)(2,1)S(1)}, u32[]{:S(2)}, u32[]{:S(2)}) collective-permute-start(bf16[768,8]{0,1:T(8,128)(2,1)S(1)} %get-tuple-element.41), channel_id=1, source_target_pairs={{0,7},{1,8},{2,9},{3,10},{4,11},{5,12},{6,13},{7,14},{8,15},{9,16}... | collective-permute-start | bytes 36872
  235.7 16.9 %collective-permute-start.49 = (bf16[768,8]{0,1:T(8,128)(2,1)S(1)}, bf16[768,8]{0,1:T(8,128)(2,1)S(1)}, u32[]{:S(2)}, u32[]{:S(2)}) collective-permute-start(bf16[768,8]{0,1:T(8,128)(2,1)S(1)} %get-tuple-element.41), channel_id=1, source_target_pairs={{0,6},{1,7},{2,8},{3,9},{4,10},{5,11},{6,12},{7,13},{8,14},{9,15},... | collective-permute-start | bytes 36872
  237.7 16.9 %collective-permute-start.48 = (bf16[768,8]{0,1:T(8,128)(2,1)S(1)}, bf16[768,8]{0,1:T(8,128)(2,1)S(1)}, u32[]{:S(2)}, u32[]{:S(2)}) collective-permute-start(bf16[768,8]{0,1:T(8,128)(2,1)S(1)} %get-tuple-element.41), channel_id=1, source_target_pairs={{0,5},{1,6},{2,7},{3,8},{4,9},{5,10},{6,11},{7,12},{8,13},{9,14},{... | collective-permute-start | bytes 36872
  239.6 17.2 %collective-permute-start.47 = (bf16[768,8]{0,1:T(8,128)(2,1)S(1)}, bf16[768,8]{0,1:T(8,128)(2,1)S(1)}, u32[]{:S(2)}, u32[]{:S(2)}) collective-permute-start(bf16[768,8]{0,1:T(8,128)(2,1)S(1)} %get-tuple-element.41), channel_id=1, source_target_pairs={{0,4},{1,5},{2,6},{3,7},{4,8},{5,9},{6,10},{7,11},{8,12},{9,13},{1... | collective-permute-start | bytes 36872
  241.5 17.2 %collective-permute-start.46 = (bf16[768,8]{0,1:T(8,128)(2,1)S(1)}, bf16[768,8]{0,1:T(8,128)(2,1)S(1)}, u32[]{:S(2)}, u32[]{:S(2)}) collective-permute-start(bf16[768,8]{0,1:T(8,128)(2,1)S(1)} %get-tuple-element.41), channel_id=1, source_target_pairs={{0,3},{1,4},{2,5},{3,6},{4,7},{5,8},{6,9},{7,10},{8,11},{9,12},{10... | collective-permute-start | bytes 36872
  250.7 19.8 %collective-permute-start.58 = (bf16[768,8]{0,1:T(8,128)(2,1)S(1)}, bf16[768,8]{0,1:T(8,128)(2,1)S(1)}, u32[]{:S(2)}, u32[]{:S(2)}) collective-permute-start(bf16[768,8]{0,1:T(8,128)(2,1)S(1)} %get-tuple-element.40), channel_id=1, source_target_pairs={{0,7},{1,8},{2,9},{3,10},{4,11},{5,12},{6,13},{7,14},{8,15},{9,16}... | collective-permute-start | bytes 36872
  252.6 21.2 %collective-permute-start.57 = (bf16[768,8]{0,1:T(8,128)(2,1)S(1)}, bf16[768,8]{0,1:T(8,128)(2,1)S(1)}, u32[]{:S(2)}, u32[]{:S(2)}) collective-permute-start(bf16[768,8]{0,1:T(8,128)(2,1)S(1)} %get-tuple-element.40), channel_id=1, source_target_pairs={{0,6},{1,7},{2,8},{3,9},{4,10},{5,11},{6,12},{7,13},{8,14},{9,15},... | collective-permute-start | bytes 36872
  254.5 8.0 %collective-permute-start.45 = (bf16[768,8]{0,1:T(8,128)(2,1)S(1)}, bf16[768,8]{0,1:T(8,128)(2,1)S(1)}, u32[]{:S(2)}, u32[]{:S(2)}) collective-permute-start(bf16[768,8]{0,1:T(8,128)(2,1)S(1)} %get-tuple-element.41), channel_id=1, source_target_pairs={{0,2},{1,3},{2,4},{3,5},{4,6},{5,7},{6,8},{7,9},{8,10},{9,11},{10,... | collective-permute-start | bytes 36872
  256.8 7.7 %collective-permute-start.44 = (bf16[768,8]{0,1:T(8,128)(2,1)S(1)}, bf16[768,8]{0,1:T(8,128)(2,1)S(1)}, u32[]{:S(2)}, u32[]{:S(2)}) collective-permute-start(bf16[768,8]{0,1:T(8,128)(2,1)S(1)} %get-tuple-element.41), channel_id=1, source_target_pairs={{0,1},{1,2},{2,3},{3,4},{4,5},{5,6},{6,7},{7,8},{8,9},{9,10},{10,1... | collective-permute-start | bytes 36872
  258.7 8.6 %collective-permute-start.59 = (bf16[768,6]{0,1:T(8,128)(2,1)S(1)}, bf16[768,6]{0,1:T(8,128)(2,1)S(1)}, u32[]{:S(2)}, u32[]{:S(2)}) collective-permute-start(bf16[768,6]{0,1:T(8,128)(2,1)S(1)} %slice.213), channel_id=1, source_target_pairs={{0,8},{1,9},{2,10},{3,11},{4,12},{5,13},{6,14},{7,15},{8,16},{9,17... | collective-permute-start | bytes 27656
  262.5 14.2 %collective-permute-start.56 = (bf16[768,8]{0,1:T(8,128)(2,1)S(1)}, bf16[768,8]{0,1:T(8,128)(2,1)S(1)}, u32[]{:S(2)}, u32[]{:S(2)}) collective-permute-start(bf16[768,8]{0,1:T(8,128)(2,1)S(1)} %get-tuple-element.40), channel_id=1, source_target_pairs={{0,5},{1,6},{2,7},{3,8},{4,9},{5,10},{6,11},{7,12},{8,13},{9,14},{... | collective-permute-start | bytes 36872
  264.5 12.2 %collective-permute-start.55 = (bf16[768,8]{0,1:T(8,128)(2,1)S(1)}, bf16[768,8]{0,1:T(8,128)(2,1)S(1)}, u32[]{:S(2)}, u32[]{:S(2)}) collective-permute-start(bf16[768,8]{0,1:T(8,128)(2,1)S(1)} %get-tuple-element.40), channel_id=1, source_target_pairs={{0,4},{1,5},{2,6},{3,7},{4,8},{5,9},{6,10},{7,11},{8,12},{9,13},{1... | collective-permute-start | bytes 36872
  267.3 9.4 %collective-permute-start.54 = (bf16[768,8]{0,1:T(8,128)(2,1)S(1)}, bf16[768,8]{0,1:T(8,128)(2,1)S(1)}, u32[]{:S(2)}, u32[]{:S(2)}) collective-permute-start(bf16[768,8]{0,1:T(8,128)(2,1)S(1)} %get-tuple-element.40), channel_id=1, source_target_pairs={{0,3},{1,4},{2,5},{3,6},{4,7},{5,8},{6,9},{7,10},{8,11},{9,12},{10... | collective-permute-start | bytes 36872
  270.5 8.0 %collective-permute-start.53 = (bf16[768,8]{0,1:T(8,128)(2,1)S(1)}, bf16[768,8]{0,1:T(8,128)(2,1)S(1)}, u32[]{:S(2)}, u32[]{:S(2)}) collective-permute-start(bf16[768,8]{0,1:T(8,128)(2,1)S(1)} %get-tuple-element.40), channel_id=1, source_target_pairs={{0,2},{1,3},{2,4},{3,5},{4,6},{5,7},{6,8},{7,9},{8,10},{9,11},{10,... | collective-permute-start | bytes 36872
  273.8 7.4 %collective-permute-start.52 = (bf16[768,8]{0,1:T(8,128)(2,1)S(1)}, bf16[768,8]{0,1:T(8,128)(2,1)S(1)}, u32[]{:S(2)}, u32[]{:S(2)}) collective-permute-start(bf16[768,8]{0,1:T(8,128)(2,1)S(1)} %get-tuple-element.40), channel_id=1, source_target_pairs={{0,1},{1,2},{2,3},{3,4},{4,5},{5,6},{6,7},{7,8},{8,9},{9,10},{10,1... | collective-permute-start | bytes 36872
  276.6 298.1 %reduce-scatter.33.cloned.1.call-start = ((), (), s32[]{:S(2)}) async-start(), calls=%async_computation.7 | async-start | bytes 208896
  283.1 293.1 %reduce-scatter.29.cloned.1.call-start = ((), (), s32[]{:S(2)}) async-start(), calls=%async_computation.5 | async-start | bytes 405504 | tf_op jit(solution)/shard_map/reduce_scatter | solution.py:241
  284.8 381.2 %reduce-scatter.27.cloned.1.call-start = ((), (), s32[]{:S(2)}) async-start(), calls=%async_computation.4 | async-start | bytes 405504 | tf_op jit(solution)/shard_map/reduce_scatter | solution.py:241
  286.0 135.0 %collective-permute-start.42 = (bf16[192,8]{0,1:T(8,128)(2,1)S(1)}, bf16[192,8]{0,1:T(8,128)(2,1)S(1)}, u32[]{:S(2)}, u32[]{:S(2)}) collective-permute-start(bf16[192,8]{0,1:T(8,128)(2,1)S(1)} %get-tuple-element.38), channel_id=1, source_target_pairs={{0,7},{1,8},{2,9},{3,10},{4,11},{5,12},{6,13},{7,14},{8,15},{9,16}... | collective-permute-start | bytes 9224
  288.1 139.7 %collective-permute-start.41 = (bf16[192,8]{0,1:T(8,128)(2,1)S(1)}, bf16[192,8]{0,1:T(8,128)(2,1)S(1)}, u32[]{:S(2)}, u32[]{:S(2)}) collective-permute-start(bf16[192,8]{0,1:T(8,128)(2,1)S(1)} %get-tuple-element.38), channel_id=1, source_target_pairs={{0,6},{1,7},{2,8},{3,9},{4,10},{5,11},{6,12},{7,13},{8,14},{9,15},... | collective-permute-start | bytes 9224
  290.0 141.8 %collective-permute-start.40 = (bf16[192,8]{0,1:T(8,128)(2,1)S(1)}, bf16[192,8]{0,1:T(8,128)(2,1)S(1)}, u32[]{:S(2)}, u32[]{:S(2)}) collective-permute-start(bf16[192,8]{0,1:T(8,128)(2,1)S(1)} %get-tuple-element.38), channel_id=1, source_target_pairs={{0,5},{1,6},{2,7},{3,8},{4,9},{5,10},{6,11},{7,12},{8,13},{9,14},{... | collective-permute-start | bytes 9224
  293.1 7.9 %collective-permute-start.35 = (bf16[192,6]{0,1:T(8,128)(2,1)S(1)}, bf16[192,6]{0,1:T(8,128)(2,1)S(1)}, u32[]{:S(2)}, u32[]{:S(2)}) collective-permute-start(bf16[192,6]{0,1:T(8,128)(2,1)S(1)} %slice.210), channel_id=1, source_target_pairs={{0,8},{1,9},{2,10},{3,11},{4,12},{5,13},{6,14},{7,15},{8,16},{9,17... | collective-permute-start | bytes 6920
  295.1 7.8 %collective-permute-start.43 = (bf16[192,6]{0,1:T(8,128)(2,1)S(1)}, bf16[192,6]{0,1:T(8,128)(2,1)S(1)}, u32[]{:S(2)}, u32[]{:S(2)}) collective-permute-start(bf16[192,6]{0,1:T(8,128)(2,1)S(1)} %slice.211), channel_id=1, source_target_pairs={{0,8},{1,9},{2,10},{3,11},{4,12},{5,13},{6,14},{7,15},{8,16},{9,17... | collective-permute-start | bytes 6920
  301.0 146.0 %collective-permute-start.39 = (bf16[192,8]{0,1:T(8,128)(2,1)S(1)}, bf16[192,8]{0,1:T(8,128)(2,1)S(1)}, u32[]{:S(2)}, u32[]{:S(2)}) collective-permute-start(bf16[192,8]{0,1:T(8,128)(2,1)S(1)} %get-tuple-element.38), channel_id=1, source_target_pairs={{0,4},{1,5},{2,6},{3,7},{4,8},{5,9},{6,10},{7,11},{8,12},{9,13},{1... | collective-permute-start | bytes 9224
  302.9 146.3 %collective-permute-start.38 = (bf16[192,8]{0,1:T(8,128)(2,1)S(1)}, bf16[192,8]{0,1:T(8,128)(2,1)S(1)}, u32[]{:S(2)}, u32[]{:S(2)}) collective-permute-start(bf16[192,8]{0,1:T(8,128)(2,1)S(1)} %get-tuple-element.38), channel_id=1, source_target_pairs={{0,3},{1,4},{2,5},{3,6},{4,7},{5,8},{6,9},{7,10},{8,11},{9,12},{10... | collective-permute-start | bytes 9224
  421.1 94.2 %collective-permute-start.37 = (bf16[192,8]{0,1:T(8,128)(2,1)S(1)}, bf16[192,8]{0,1:T(8,128)(2,1)S(1)}, u32[]{:S(2)}, u32[]{:S(2)}) collective-permute-start(bf16[192,8]{0,1:T(8,128)(2,1)S(1)} %get-tuple-element.38), channel_id=1, source_target_pairs={{0,2},{1,3},{2,4},{3,5},{4,6},{5,7},{6,8},{7,9},{8,10},{9,11},{10,... | collective-permute-start | bytes 9224
  427.9 89.3 %collective-permute-start.36 = (bf16[192,8]{0,1:T(8,128)(2,1)S(1)}, bf16[192,8]{0,1:T(8,128)(2,1)S(1)}, u32[]{:S(2)}, u32[]{:S(2)}) collective-permute-start(bf16[192,8]{0,1:T(8,128)(2,1)S(1)} %get-tuple-element.38), channel_id=1, source_target_pairs={{0,1},{1,2},{2,3},{3,4},{4,5},{5,6},{6,7},{7,8},{8,9},{9,10},{10,1... | collective-permute-start | bytes 9224
  431.8 87.3 %collective-permute-start.34 = (bf16[192,8]{0,1:T(8,128)(2,1)S(1)}, bf16[192,8]{0,1:T(8,128)(2,1)S(1)}, u32[]{:S(2)}, u32[]{:S(2)}) collective-permute-start(bf16[192,8]{0,1:T(8,128)(2,1)S(1)} %get-tuple-element.39), channel_id=1, source_target_pairs={{0,7},{1,8},{2,9},{3,10},{4,11},{5,12},{6,13},{7,14},{8,15},{9,16}... | collective-permute-start | bytes 9224
  447.0 76.2 %collective-permute-start.33 = (bf16[192,8]{0,1:T(8,128)(2,1)S(1)}, bf16[192,8]{0,1:T(8,128)(2,1)S(1)}, u32[]{:S(2)}, u32[]{:S(2)}) collective-permute-start(bf16[192,8]{0,1:T(8,128)(2,1)S(1)} %get-tuple-element.39), channel_id=1, source_target_pairs={{0,6},{1,7},{2,8},{3,9},{4,10},{5,11},{6,12},{7,13},{8,14},{9,15},... | collective-permute-start | bytes 9224
  449.2 75.9 %collective-permute-start.32 = (bf16[192,8]{0,1:T(8,128)(2,1)S(1)}, bf16[192,8]{0,1:T(8,128)(2,1)S(1)}, u32[]{:S(2)}, u32[]{:S(2)}) collective-permute-start(bf16[192,8]{0,1:T(8,128)(2,1)S(1)} %get-tuple-element.39), channel_id=1, source_target_pairs={{0,5},{1,6},{2,7},{3,8},{4,9},{5,10},{6,11},{7,12},{8,13},{9,14},{... | collective-permute-start | bytes 9224
  515.2 13.2 %collective-permute-start.31 = (bf16[192,8]{0,1:T(8,128)(2,1)S(1)}, bf16[192,8]{0,1:T(8,128)(2,1)S(1)}, u32[]{:S(2)}, u32[]{:S(2)}) collective-permute-start(bf16[192,8]{0,1:T(8,128)(2,1)S(1)} %get-tuple-element.39), channel_id=1, source_target_pairs={{0,4},{1,5},{2,6},{3,7},{4,8},{5,9},{6,10},{7,11},{8,12},{9,13},{1... | collective-permute-start | bytes 9224
  517.2 14.9 %collective-permute-start.30 = (bf16[192,8]{0,1:T(8,128)(2,1)S(1)}, bf16[192,8]{0,1:T(8,128)(2,1)S(1)}, u32[]{:S(2)}, u32[]{:S(2)}) collective-permute-start(bf16[192,8]{0,1:T(8,128)(2,1)S(1)} %get-tuple-element.39), channel_id=1, source_target_pairs={{0,3},{1,4},{2,5},{3,6},{4,7},{5,8},{6,9},{7,10},{8,11},{9,12},{10... | collective-permute-start | bytes 9224
  519.1 14.9 %collective-permute-start.29 = (bf16[192,8]{0,1:T(8,128)(2,1)S(1)}, bf16[192,8]{0,1:T(8,128)(2,1)S(1)}, u32[]{:S(2)}, u32[]{:S(2)}) collective-permute-start(bf16[192,8]{0,1:T(8,128)(2,1)S(1)} %get-tuple-element.39), channel_id=1, source_target_pairs={{0,2},{1,3},{2,4},{3,5},{4,6},{5,7},{6,8},{7,9},{8,10},{9,11},{10,... | collective-permute-start | bytes 9224
  523.2 12.8 %collective-permute-start.28 = (bf16[192,8]{0,1:T(8,128)(2,1)S(1)}, bf16[192,8]{0,1:T(8,128)(2,1)S(1)}, u32[]{:S(2)}, u32[]{:S(2)}) collective-permute-start(bf16[192,8]{0,1:T(8,128)(2,1)S(1)} %get-tuple-element.39), channel_id=1, source_target_pairs={{0,1},{1,2},{2,3},{3,4},{4,5},{5,6},{6,7},{7,8},{8,9},{9,10},{10,1... | collective-permute-start | bytes 9224
  525.1 12.8 %collective-permute-start.27 = (bf16[192,18]{0,1:T(8,128)(2,1)S(1)}, bf16[192,18]{0,1:T(8,128)(2,1)S(1)}, u32[]{:S(2)}, u32[]{:S(2)}) collective-permute-start(bf16[192,18]{0,1:T(8,128)(2,1)S(1)} %slice.209), channel_id=1, source_target_pairs={{0,8},{1,9},{2,10},{3,11},{4,12},{5,13},{6,14},{7,15},{8,16},{9,17... | collective-permute-start | bytes 20744
  528.5 13.2 %collective-permute-start.26 = (bf16[192,24]{0,1:T(8,128)(2,1)S(1)}, bf16[192,24]{0,1:T(8,128)(2,1)S(1)}, u32[]{:S(2)}, u32[]{:S(2)}) collective-permute-start(bf16[192,24]{0,1:T(8,128)(2,1)S(1)} %get-tuple-element.36), channel_id=1, source_target_pairs={{0,7},{1,8},{2,9},{3,10},{4,11},{5,12},{6,13},{7,14},{8,15},{9,16}... | collective-permute-start | bytes 27656
  532.1 13.2 %collective-permute-start.25 = (bf16[192,24]{0,1:T(8,128)(2,1)S(1)}, bf16[192,24]{0,1:T(8,128)(2,1)S(1)}, u32[]{:S(2)}, u32[]{:S(2)}) collective-permute-start(bf16[192,24]{0,1:T(8,128)(2,1)S(1)} %get-tuple-element.36), channel_id=1, source_target_pairs={{0,6},{1,7},{2,8},{3,9},{4,10},{5,11},{6,12},{7,13},{8,14},{9,15},... | collective-permute-start | bytes 27656
  534.0 13.2 %collective-permute-start.24 = (bf16[192,24]{0,1:T(8,128)(2,1)S(1)}, bf16[192,24]{0,1:T(8,128)(2,1)S(1)}, u32[]{:S(2)}, u32[]{:S(2)}) collective-permute-start(bf16[192,24]{0,1:T(8,128)(2,1)S(1)} %get-tuple-element.36), channel_id=1, source_target_pairs={{0,5},{1,6},{2,7},{3,8},{4,9},{5,10},{6,11},{7,12},{8,13},{9,14},{... | collective-permute-start | bytes 27656
  536.0 13.2 %collective-permute-start.23 = (bf16[192,24]{0,1:T(8,128)(2,1)S(1)}, bf16[192,24]{0,1:T(8,128)(2,1)S(1)}, u32[]{:S(2)}, u32[]{:S(2)}) collective-permute-start(bf16[192,24]{0,1:T(8,128)(2,1)S(1)} %get-tuple-element.36), channel_id=1, source_target_pairs={{0,4},{1,5},{2,6},{3,7},{4,8},{5,9},{6,10},{7,11},{8,12},{9,13},{1... | collective-permute-start | bytes 27656
  537.9 13.5 %collective-permute-start.22 = (bf16[192,24]{0,1:T(8,128)(2,1)S(1)}, bf16[192,24]{0,1:T(8,128)(2,1)S(1)}, u32[]{:S(2)}, u32[]{:S(2)}) collective-permute-start(bf16[192,24]{0,1:T(8,128)(2,1)S(1)} %get-tuple-element.36), channel_id=1, source_target_pairs={{0,3},{1,4},{2,5},{3,6},{4,7},{5,8},{6,9},{7,10},{8,11},{9,12},{10... | collective-permute-start | bytes 27656
  541.7 11.6 %collective-permute-start.21 = (bf16[192,24]{0,1:T(8,128)(2,1)S(1)}, bf16[192,24]{0,1:T(8,128)(2,1)S(1)}, u32[]{:S(2)}, u32[]{:S(2)}) collective-permute-start(bf16[192,24]{0,1:T(8,128)(2,1)S(1)} %get-tuple-element.36), channel_id=1, source_target_pairs={{0,2},{1,3},{2,4},{3,5},{4,6},{5,7},{6,8},{7,9},{8,10},{9,11},{10,... | collective-permute-start | bytes 27656
  545.3 10.3 %collective-permute-start.20 = (bf16[192,24]{0,1:T(8,128)(2,1)S(1)}, bf16[192,24]{0,1:T(8,128)(2,1)S(1)}, u32[]{:S(2)}, u32[]{:S(2)}) collective-permute-start(bf16[192,24]{0,1:T(8,128)(2,1)S(1)} %get-tuple-element.36), channel_id=1, source_target_pairs={{0,1},{1,2},{2,3},{3,4},{4,5},{5,6},{6,7},{7,8},{8,9},{9,10},{10,1... | collective-permute-start | bytes 27656
  547.2 14.6 %collective-permute-start.18 = (bf16[192,24]{0,1:T(8,128)(2,1)S(1)}, bf16[192,24]{0,1:T(8,128)(2,1)S(1)}, u32[]{:S(2)}, u32[]{:S(2)}) collective-permute-start(bf16[192,24]{0,1:T(8,128)(2,1)S(1)} %get-tuple-element.37), channel_id=1, source_target_pairs={{0,7},{1,8},{2,9},{3,10},{4,11},{5,12},{6,13},{7,14},{8,15},{9,16}... | collective-permute-start | bytes 27656
  549.1 16.3 %collective-permute-start.17 = (bf16[192,24]{0,1:T(8,128)(2,1)S(1)}, bf16[192,24]{0,1:T(8,128)(2,1)S(1)}, u32[]{:S(2)}, u32[]{:S(2)}) collective-permute-start(bf16[192,24]{0,1:T(8,128)(2,1)S(1)} %get-tuple-element.37), channel_id=1, source_target_pairs={{0,6},{1,7},{2,8},{3,9},{4,10},{5,11},{6,12},{7,13},{8,14},{9,15},... | collective-permute-start | bytes 27656
  551.4 8.5 %collective-permute-start.19 = (bf16[192,18]{0,1:T(8,128)(2,1)S(1)}, bf16[192,18]{0,1:T(8,128)(2,1)S(1)}, u32[]{:S(2)}, u32[]{:S(2)}) collective-permute-start(bf16[192,18]{0,1:T(8,128)(2,1)S(1)} %slice.208), channel_id=1, source_target_pairs={{0,8},{1,9},{2,10},{3,11},{4,12},{5,13},{6,14},{7,15},{8,16},{9,17... | collective-permute-start | bytes 20744
  553.3 14.1 %collective-permute-start.16 = (bf16[192,24]{0,1:T(8,128)(2,1)S(1)}, bf16[192,24]{0,1:T(8,128)(2,1)S(1)}, u32[]{:S(2)}, u32[]{:S(2)}) collective-permute-start(bf16[192,24]{0,1:T(8,128)(2,1)S(1)} %get-tuple-element.37), channel_id=1, source_target_pairs={{0,5},{1,6},{2,7},{3,8},{4,9},{5,10},{6,11},{7,12},{8,13},{9,14},{... | collective-permute-start | bytes 27656
  555.5 11.9 %collective-permute-start.15 = (bf16[192,24]{0,1:T(8,128)(2,1)S(1)}, bf16[192,24]{0,1:T(8,128)(2,1)S(1)}, u32[]{:S(2)}, u32[]{:S(2)}) collective-permute-start(bf16[192,24]{0,1:T(8,128)(2,1)S(1)} %get-tuple-element.37), channel_id=1, source_target_pairs={{0,4},{1,5},{2,6},{3,7},{4,8},{5,9},{6,10},{7,11},{8,12},{9,13},{1... | collective-permute-start | bytes 27656
  559.9 7.5 %collective-permute-start.14 = (bf16[192,24]{0,1:T(8,128)(2,1)S(1)}, bf16[192,24]{0,1:T(8,128)(2,1)S(1)}, u32[]{:S(2)}, u32[]{:S(2)}) collective-permute-start(bf16[192,24]{0,1:T(8,128)(2,1)S(1)} %get-tuple-element.37), channel_id=1, source_target_pairs={{0,3},{1,4},{2,5},{3,6},{4,7},{5,8},{6,9},{7,10},{8,11},{9,12},{10... | collective-permute-start | bytes 27656
  561.8 8.0 %collective-permute-start.13 = (bf16[192,24]{0,1:T(8,128)(2,1)S(1)}, bf16[192,24]{0,1:T(8,128)(2,1)S(1)}, u32[]{:S(2)}, u32[]{:S(2)}) collective-permute-start(bf16[192,24]{0,1:T(8,128)(2,1)S(1)} %get-tuple-element.37), channel_id=1, source_target_pairs={{0,2},{1,3},{2,4},{3,5},{4,6},{5,7},{6,8},{7,9},{8,10},{9,11},{10,... | collective-permute-start | bytes 27656
  565.4 7.4 %collective-permute-start.12 = (bf16[192,24]{0,1:T(8,128)(2,1)S(1)}, bf16[192,24]{0,1:T(8,128)(2,1)S(1)}, u32[]{:S(2)}, u32[]{:S(2)}) collective-permute-start(bf16[192,24]{0,1:T(8,128)(2,1)S(1)} %get-tuple-element.37), channel_id=1, source_target_pairs={{0,1},{1,2},{2,3},{3,4},{4,5},{5,6},{6,7},{7,8},{8,9},{9,10},{10,1... | collective-permute-start | bytes 27656
  (72 other events, 882.6 us)
Sparse Core Ops, SparseCore 0:
  276.8 76.2 reduce-scatter.30
  355.8 69.9 reduce-scatter.32
  430.4 114.2 reduce-scatter.28
  549.1 116.8 reduce-scatter.26
